TPU v7x, 128 devices: a whole 4x4x4 slice. The times are simulated.
128 devices in a mesh: lon: 16 (over y_hi, x, core), lat: 8 (over y_lo, z).
Axes of the slice: x: 4, y: 4 (y_hi: 2, y_lo: 2; y = y_hi * 2 + y_lo), z: 4, core: 2. Of those that a mesh axis runs over, the one named last changes fastest.
Arguments:
- grid_state: bfloat16 [1024, 256, 384], P('lon', 'lat'), may hold values from -6 to 6
- conv_weight: bfloat16 [9, 384, 384], replicated, may hold values from -0.109375 to 0.109375
- mix_weight: bfloat16 [384, 384], replicated, may hold values from -0.3125 to 0.3125
- teacher: bfloat16 [8, 128, 256, 384], P('lat', 'lon'), may hold values from -6 to 6
- tile_mask: int32 [16, 8, 8], P('lon', 'lat'), may hold values from 0 to 1, as said below
- source_owner: int32 [8, 16, 16], P('lat'), may hold values from 0 to 15, as said below
- source_block: int32 [8, 16, 16], P('lat'), may hold values from 0 to 7
- margin_weight: float32 [8, 16, 16], P('lat', 'lon'), may hold values from 0.2 to 1
Outputs:
- next_state: bfloat16 [1024, 256, 384], P('lon', 'lat')
- misfit: bfloat16 [1024, 256, 384], P('lon', 'lat')
- grad_conv: float32 [9, 384, 384], replicated
- grad_mix: float32 [384, 384], replicated
Inputs may be any that keep to these rules, and one draw needn't show every extreme that they name: `tile_mask`: 1 marks an ocean tile; every device holds 1 to 4 ocean tiles, and some device holds exactly 4. `source_owner`: blocks lie in the tile's own latitude row. Among the 16 entries of one device no lon index appears more than 2 times, and on every device some lon index appears exactly 2 times.
All inputs are finite; a program needn't handle non-finite values.
Results may differ from a plain program's by a relative error of at most 0.0032.
Values may be sent and summed in bfloat16 or wider, within the bound.
A program may use at most 128 MiB of HBM per device.

v0:
```python
import math

import jax
import jax.numpy as jnp
from jax import lax
from jax.sharding import PartitionSpec as P

TS = 16
K = 2


def with_halo(cells, sides, width, closed):
    for axis, dim in sides:
        count = lax.axis_size(axis)
        ends = count if closed else count - 1
        head = lax.slice_in_dim(cells, 0, width, axis=dim)
        tail = lax.slice_in_dim(cells, cells.shape[dim] - width, cells.shape[dim], axis=dim)
        cells = jnp.concatenate(
            [
                lax.ppermute(tail, axis, [(i, (i + 1) % count) for i in range(ends)]),
                cells,
                lax.ppermute(head, axis, [((i + 1) % count, i) for i in range(ends)]),
            ],
            axis=dim,
        )
    return cells


def block_step(windows, centre, target, keep_rows, conv_weight, mix_weight, scale):
    count, height, breadth, chans = windows.shape
    height = height - 2
    breadth = breadth - 2
    row_count = count * height * breadth

    def shifted(offset):
        step_lon, step_lat = divmod(offset, 3)
        return windows[:, step_lon : step_lon + height, step_lat : step_lat + breadth, :].reshape(
            row_count, chans
        )

    pre = jnp.zeros((row_count, chans), jnp.float32)
    for offset in range(9):
        pre = pre + jnp.dot(
            shifted(offset), conv_weight[offset], preferred_element_type=jnp.float32
        )
    sigmoid_pre = jax.nn.sigmoid(pre)
    hidden = (pre * sigmoid_pre).astype(jnp.bfloat16)
    full_state = centre.astype(jnp.float32) + jnp.dot(
        hidden, mix_weight, preferred_element_type=jnp.float32
    )
    next_state = (keep_rows * full_state).astype(jnp.bfloat16)
    error = keep_rows * (full_state - target)
    misfit = error.astype(jnp.bfloat16)
    scaled = (error * scale).astype(jnp.bfloat16)
    grad_mix = lax.dot_general(
        hidden, scaled, (((0,), (0,)), ((), ())), preferred_element_type=jnp.float32
    )
    back_grad = lax.dot_general(
        scaled, mix_weight, (((1,), (1,)), ((), ())), preferred_element_type=jnp.float32
    )
    dpre = (back_grad * sigmoid_pre * (1.0 + pre * (1.0 - sigmoid_pre))).astype(jnp.bfloat16)
    grad_conv = jnp.stack(
        [
            lax.dot_general(
                shifted(offset), dpre, (((0,), (0,)), ((), ())), preferred_element_type=jnp.float32
            )
            for offset in range(9)
        ]
    )
    return (next_state, misfit, grad_conv, grad_mix)


def tiles_to_block(tiles, tiles_lon, tiles_lat, side):
    chans = tiles.shape[-1]
    shaped = tiles.reshape(tiles_lon, tiles_lat, side, side, chans)
    return jnp.transpose(shaped, (0, 2, 1, 3, 4)).reshape(tiles_lon * side, tiles_lat * side, chans)


def body(
    grid_state,
    conv_weight,
    mix_weight,
    teacher,
    tile_mask,
    source_owner,
    source_block,
    margin_weight,
):
    lon_count = lax.axis_size("lon")
    lat_count = lax.axis_size("lat")
    my_lon = lax.axis_index("lon")
    width_lon, width_lat, chans = grid_state.shape
    side = TS
    tiles_lon = width_lon // side
    tiles_lat = width_lat // side
    tile_count = tiles_lon * tiles_lat
    cells_tile = side * side
    owners = source_owner[0]
    blocks = source_block[0]
    my_owner = lax.dynamic_index_in_dim(owners, my_lon, 0, keepdims=False)
    my_block = lax.dynamic_index_in_dim(blocks, my_lon, 0, keepdims=False)
    local_blocks = teacher[0]
    held = local_blocks.shape[0]
    wanted = my_owner * held + my_block
    piece = lax.all_gather(local_blocks, "lon", axis=0, tiled=True)
    rows_here = jnp.arange(piece.shape[0], dtype=jnp.int32)
    pick_rows = (wanted[:, None] == rows_here[None, :]).astype(jnp.bfloat16)
    picked = jnp.einsum("rj,jcx->rcx", pick_rows, piece, preferred_element_type=jnp.float32)
    weights = margin_weight[0, 0]
    mixed = picked * weights[:, None, None]
    target_tiles = jnp.sum(mixed.reshape(tile_count, K, cells_tile, chans), axis=1)
    lon_wide = with_halo(grid_state, (("lon", 0),), 1, True)
    padded = with_halo(lon_wide, (("lat", 1),), 1, False)
    scale = 1.0 / math.sqrt(width_lon * lon_count * width_lat * lat_count)
    ocean_tiles = tile_mask[0, 0]
    ocean_grid = ocean_tiles.astype(jnp.float32).reshape(tiles_lon, tiles_lat)
    keep_rows = jnp.broadcast_to(
        ocean_grid[:, None, :, None], (tiles_lon, side, tiles_lat, side)
    ).reshape(width_lon * width_lat, 1)
    target_rows = tiles_to_block(target_tiles, tiles_lon, tiles_lat, side).reshape(
        width_lon * width_lat, chans
    )
    next_rows, misfit_rows, grad_conv, grad_mix = block_step(
        padded[None],
        grid_state.reshape(width_lon * width_lat, chans),
        target_rows,
        keep_rows,
        conv_weight,
        mix_weight,
        scale,
    )
    next_state = next_rows.reshape(width_lon, width_lat, chans)
    misfit = misfit_rows.reshape(width_lon, width_lat, chans)
    grad_conv, grad_mix = lax.psum((grad_conv, grad_mix), ("lon", "lat"))
    return (next_state, misfit, grad_conv, grad_mix)


def solution(mesh):
    in_specs = (
        P("lon", "lat", None),
        P(),
        P(),
        P("lat", "lon", None, None),
        P("lon", "lat", None),
        P("lat", None, None),
        P("lat", None, None),
        P("lat", "lon", None),
    )
    out_specs = (P("lon", "lat", None), P("lon", "lat", None), P(), P())
    return jax.shard_map(body, mesh=mesh, in_specs=in_specs, out_specs=out_specs, check_vma=False)
```

profile of v0, /device:TPU:1, one launch (start us, length us, event | category | flops | bytes accessed | tf_op | source)
XLA Modules:
  0.0 407.1 jit_solution(4890446071105545086)
XLA Ops:
  7.2 3.6 copy.15
  11.5 1.4 collective-permute-start.1
  13.0 1.2 collective-permute-start
  14.2 4.4 %collective-permute-done = bf16[1,32,384]{2,1,0:T(8,128)(2,1)S(1)} collective-permute-done((bf16[1,32,384]{2,1,0:T(8,128)(2,1)S(1)}, bf16[1,32,384]{2,1,0:T(8,128)(2,1)S(1)}, u32[]{:S(2)}, u32[]{:S(2)}) %collective-permute-start) | collective-permute-done | bytes 24608 | tf_op jit(solution)/shard_map/ppermute | solution.py:20
  19.1 3.5 collective-permute-start.2
  22.6 1.3 collective-permute-start.3
  25.0 3.2 collective-permute-done.3
  28.2 1.3 maximum_bitcast_fusion
  29.5 4.6 %fusion.48 = (bf16[1,64,32,384]{3,2,1,0:T(8,128)(2,1)}, bf16[1,64,32,384]{3,2,1,0:T(8,128)(2,1)S(1)}, bf16[1,64,32,384]{3,2,1,0:T(8,128)(2,1)S(1)}, bf16[1,64,32...) fusion(bf16[1,66,34,384]{3,2,1,0:T(8,128)(2,1)S(1)} %maximum_bi, ...), kind=kLoop, calls=%fused_computation.69 | loop fusion | bytes 28311552 | tf_op jit(solution)/shard_map/slice | solution.py:37
  34.2 2.5 fusion.16
  36.7 1.5 copy-done.19
  40.4 1.1 fusion.22
  46.3 4.9 %add_add_fusion = f32[2048,384]{1,0:T(8,128)} fusion(f32[2048,384]{1,0:T(8,128)S(1)} %fusion.16, f32[2048,384]{1,0:T(8,128)S(1)} %fusion.18, f32[2048,384]{1,0:T(8,128)S(1)} %fusion.20, f32[2048,384]{1,0:T(8,128)S(1)} %fusion.22, f32[2048,384]{1,0:T(8,128)S(1)} %fusion.24, f32[2048,384]{1,0:T(8,128)S(1)} %fusion.26, f32[2048,384]{1,0:T(8,128)S(1)} %fusion.30, ...), kind=kOutput, calls=%fused_computation.11 | convolution fusion | flops 610271232 | bytes 30179328 | tf_op jit(solution)/shard_map/dot_general | solution.py:43
  51.2 130.2 %all-gather.3.cloned.1.call-done = bf16[1,128,256,384]{3,1,2,0:T(8,128)(2,1)} async-done(((bf16[1,8,256,384]{3,1,2,0:T(8,128)(2,1)}), bf16[1,128,256,384]{3,1,2,0:T(8,128)(2,1)}) %all-gather.3.cloned.1.call-update) | async-done | bytes 25165840 | tf_op jit(solution)/shard_map/all_gather | solution.py:105
  181.4 13.0 %broadcast_multiply_fusion = f32[16,256,384]{2,0,1:T(8,128)} fusion(f32[16]{0:T(128)S(1)} %bitcast.148, bf16[1,128,256,384]{3,1,2,0:T(8,128)(2,1)} %all-gather.3.cloned.1.call-done, s32[16]{0:T(128)S(1)} %add_bitcast_fusion), kind=kOutput, calls=%fused_computation.7 | convolution fusion | flops 404228096 | bytes 31457408 | tf_op jit(solution)/shard_map/rj,jcx->rcx/dot_general | solution.py:108
  194.3 8.2 %reshape.95 = f32[8,2,256,384]{3,1,0,2:T(2,128)} reshape(f32[16,256,384]{2,0,1:T(8,128)} %broadcast_multiply_fusion) | data formatting | bytes 12582912 | tf_op jit(solution)/shard_map/reshape | solution.py:111
  202.5 10.3 %reduce_sum.9 = f32[8,256,384]{2,0,1:T(8,128)S(1)} reduce(f32[8,2,256,384]{3,1,0,2:T(2,128)} %reshape.95, f32[]{:T(128)} %constant.22.clone.1), dimensions={1}, to_apply=%region_0.1 | reduce | flops 786432 | bytes 9437188 | tf_op jit(solution)/shard_map/reduce_sum | solution.py:111
  213.9 1.4 copy-done.18
  215.7 3.2 fusion.46
  219.0 1.9 fusion.14
  220.8 1.8 multiply_convert_fusion
  222.7 1.8 fusion.13
  224.5 1.8 fusion.12
  226.3 1.8 fusion.11
  228.2 1.8 fusion.10
  230.0 1.8 fusion.9
  231.8 1.8 fusion.8
  233.7 1.8 fusion.7
  235.5 1.8 fusion.6
  237.3 1.8 fusion.5
  239.2 154.5 %all-reduce.3.cloned.1.call-done = (f32[9,384,384]{2,1,0:T(8,128)}, f32[384,384]{1,0:T(8,128)}) async-done(((f32[9,384,384]{2,1,0:T(8,128)}, f32[384,384]{1,0:T(8,128)}), (f32[9,384,384]{2,1,0:T(8,128)}, f32[384,384]{1,0:T(8,128)})) %all-reduce.3.cloned.1.call-update) | async-done | bytes 5898256 | tf_op jit(solution)/shard_map/psum | solution.py:134
  393.7 5.3 %copy.30 = f32[9,384,384]{2,1,0:T(8,128)} copy(f32[9,384,384]{2,1,0:T(8,128)} %get-tuple-element.24) | data formatting | bytes 10616832
  (73 shorter events, 11.6 us)
Async XLA Ops:
  7.2 206.7 %copy-start = (bf16[384,384]{1,0:T(8,128)(2,1)S(1)}, bf16[384,384]{1,0:T(8,128)(2,1)}, u32[]{:S(2)}) copy-start(bf16[384,384]{1,0:T(8,128)(2,1)} %param.10) | copy-start | bytes 884740
  7.2 3.7 copy-start.20
  7.2 7.0 %copy-start.24 = (s32[1,1,8]{2,1,0:T(1,128)S(1)}, s32[1,1,8]{2,1,0:T(1,128)}, u32[]{:S(2)}) copy-start(s32[1,1,8]{2,1,0:T(1,128)} %param.12) | copy-start | bytes 100
  7.2 174.2 %all-gather.3.cloned.1.call-start = ((), (), s32[]{:S(2)}) async-start(), calls=%async_computation | async-start | bytes 26738688 | tf_op jit(solution)/shard_map/all_gather | solution.py:105
  10.9 382.9 %all-reduce.3.cloned.1.call-start = ((), (), s32[]{:S(2)}) async-start(), calls=%async_computation.1 | async-start | bytes 11796480 | tf_op jit(solution)/shard_map/psum | solution.py:134
  11.5 7.3 %collective-permute-start.1 = (bf16[1,32,384]{2,1,0:T(8,128)(2,1)}, bf16[1,32,384]{2,1,0:T(8,128)(2,1)S(1)}, u32[]{:S(2)}, u32[]{:S(2)}) collective-permute-start(bf16[1,32,384]{2,1,0:T(8,128)(2,1)} %get-tuple-element.20), channel_id=1, source_target_pairs={{8,0},{16,8},{24,16},{32,24},{40,32},{48,40},{56,48},{64,56},{72,6... | collective-permute-start | bytes 73736 | tf_op jit(solution)/shard_map/ppermute | solution.py:22
  13.0 5.6 %collective-permute-start = (bf16[1,32,384]{2,1,0:T(8,128)(2,1)S(1)}, bf16[1,32,384]{2,1,0:T(8,128)(2,1)S(1)}, u32[]{:S(2)}, u32[]{:S(2)}) collective-permute-start(bf16[1,32,384]{2,1,0:T(8,128)(2,1)S(1)} %get-tuple-element.21), channel_id=1, source_target_pairs={{0,8},{8,16},{16,24},{24,32},{32,40},{40,48},{48,56},{56,64},{64,7... | collective-permute-start | bytes 73736 | tf_op jit(solution)/shard_map/ppermute | solution.py:20
  19.1 5.9 %collective-permute-start.2 = (bf16[66,1,384]{2,1,0:T(2,128)(2,1)S(1)}, bf16[66,1,384]{2,1,0:T(2,128)(2,1)S(1)}, u32[]{:S(2)}, u32[]{:S(2)}) collective-permute-start(bf16[66,1,384]{2,1,0:T(2,128)(2,1)S(1)} %get-tuple-element.18), channel_id=1, source_target_pairs={{0,1},{1,2},{2,3},{3,4},{4,5},{5,6},{6,7},{8,9},{9,10},{10,11},{11... | collective-permute-start | bytes 152072 | tf_op jit(solution)/shard_map/ppermute | solution.py:20
  22.6 5.6 %collective-permute-start.3 = (bf16[66,1,384]{2,1,0:T(2,128)(2,1)S(1)}, bf16[66,1,384]{2,1,0:T(2,128)(2,1)S(1)}, u32[]{:S(2)}, u32[]{:S(2)}) collective-permute-start(bf16[66,1,384]{2,1,0:T(2,128)(2,1)S(1)} %get-tuple-element.19), channel_id=1, source_target_pairs={{1,0},{2,1},{3,2},{4,3},{5,4},{6,5},{7,6},{9,8},{10,9},{11,10},{12... | collective-permute-start | bytes 152072 | tf_op jit(solution)/shard_map/ppermute | solution.py:22
  34.1 2.6 copy-start.1
  34.1 2.6 copy-start.3
  34.1 5.2 %copy-start.5 = (bf16[1,64,32,384]{3,2,1,0:T(8,128)(2,1)}, bf16[1,64,32,384]{3,2,1,0:T(8,128)(2,1)S(1)}, u32[]{:S(2)}) copy-start(bf16[1,64,32,384]{3,2,1,0:T(8,128)(2,1)S(1)} %get-tuple-element.12) | copy-start | bytes 4718596
  34.1 6.3 %copy-start.7 = (bf16[1,64,32,384]{3,2,1,0:T(8,128)(2,1)}, bf16[1,64,32,384]{3,2,1,0:T(8,128)(2,1)S(1)}, u32[]{:S(2)}) copy-start(bf16[1,64,32,384]{3,2,1,0:T(8,128)(2,1)S(1)} %get-tuple-element.13) | copy-start | bytes 4718596
  34.1 7.4 %copy-start.9 = (bf16[1,64,32,384]{3,2,1,0:T(8,128)(2,1)}, bf16[1,64,32,384]{3,2,1,0:T(8,128)(2,1)S(1)}, u32[]{:S(2)}) copy-start(bf16[1,64,32,384]{3,2,1,0:T(8,128)(2,1)S(1)} %get-tuple-element.14) | copy-start | bytes 4718596
  34.1 8.5 %copy-start.11 = (bf16[1,64,32,384]{3,2,1,0:T(8,128)(2,1)}, bf16[1,64,32,384]{3,2,1,0:T(8,128)(2,1)S(1)}, u32[]{:S(2)}) copy-start(bf16[1,64,32,384]{3,2,1,0:T(8,128)(2,1)S(1)} %get-tuple-element.15) | copy-start | bytes 4718596
  34.1 9.6 %copy-start.13 = (bf16[1,64,32,384]{3,2,1,0:T(8,128)(2,1)}, bf16[1,64,32,384]{3,2,1,0:T(8,128)(2,1)S(1)}, u32[]{:S(2)}) copy-start(bf16[1,64,32,384]{3,2,1,0:T(8,128)(2,1)S(1)} %get-tuple-element.16) | copy-start | bytes 4718596
  34.1 4.0 copy-start.19
  43.8 1.4 copy-start.15
  46.3 135.1 %copy-start.23 = (f32[1,1,16]{2,1,0:T(1,128)S(1)}, f32[1,1,16]{2,1,0:T(1,128)}, u32[]{:S(2)}) copy-start(f32[1,1,16]{2,1,0:T(1,128)} %param.15) | copy-start | bytes 196
  213.4 1.9 copy-start.18
  213.4 2.3 copy-start.21
  220.8 1.8 copy-start.16
  222.7 1.8 copy-start.14
  224.5 1.8 copy-start.12
  226.3 1.8 copy-start.10
  228.2 1.8 copy-start.8
  230.0 1.8 copy-start.6
  231.8 1.8 copy-start.4
  233.7 1.8 copy-start.2
  235.5 1.8 copy-start.17
  393.7 5.3 %copy-start.22 = (f32[384,384]{1,0:T(8,128)S(1)}, f32[384,384]{1,0:T(8,128)}, u32[]{:S(2)}) copy-start(f32[384,384]{1,0:T(8,128)} %get-tuple-element.25) | copy-start | bytes 1769476
Sparse Core Ops, SparseCore 0:
  11.0 170.3 all-gather.2
  239.3 154.3 all-reduce.2
where the time goes:
time: 412 us; the launch traced here: 407 us
  waiting for transfers between devices  292 us (71%)
  matrix products  51.4 us (12%)
  local copies, waits for them, and re-layouts  28.7 us (7%)
  between operations  14.9 us (4%)
  other arithmetic  12.3 us (3%)
  starting transfers between devices  7.52 us (2%)
    psum x1, waiting for transfers between devices, body(): grad_conv, grad_mix = lax.psum((grad_conv, grad_mix), ('lon', 'lat'))  155 us
    all_gather x1, waiting for transfers between devices, body(): piece = lax.all_gather(local_blocks, 'lon', axis=0, tiled=True)  130 us
    dot_general x9, matrix products, block_step(): lax.dot_general(shifted(offset), dpre, (((0,), (0,)), ((), ())), preferre...  16.4 us
    dot_general x9, matrix products, block_step(): jnp.dot(shifted(offset), conv_weight[offset], preferred_element_type=jnp....  15.1 us
    unnamed x55, local copies, waits for them, and re-layouts  13.8 us
    dot_general x1, matrix products, body(): jnp.einsum('rj,jcx->rcx', pick_rows, piece, preferred_element_type=jnp.fl...  13 us
    reduce_sum x1, other arithmetic, body(): jnp.sum(mixed.reshape(tile_count, K, cells_tile, chans), axis=1)  10.3 us
  transfers between devices with their start and end apart: 6, of which 4 were waited for; matrix products, arithmetic and copies ran while one was open for 6% of the time, Pallas kernels for 0%

commit v1 on v0

v1 whole, which is shorter than its diff:
```python
import functools
import math

import jax
import jax.numpy as jnp
from jax import lax
from jax.experimental import pallas as pl
from jax.experimental.pallas import tpu as pltpu
from jax.sharding import PartitionSpec as P

TS = 16
K = 2
SLOTS = 4
C = 384
NX = 4
NCH = 4
CR = 128 // NCH
HALF = 2048
MESH = pl.DeviceIdType.MESH
F32 = jnp.float32
BF16 = jnp.bfloat16


def my_place():
    lon = lax.axis_index("lon")
    lat = lax.axis_index("lat")
    core = lax.rem(lon, 2)
    x = lax.rem(lax.div(lon, 2), 4)
    y = lax.div(lon, 8) * 2 + lax.div(lat, 4)
    z = lax.rem(lat, 4)
    return x, y, z, core


def device(x, y, z, core):
    x = lax.rem(x + 8, 4)
    y = lax.rem(y + 8, 4)
    z = lax.rem(z + 8, 4)
    return (lax.div(y, 2) * 8 + x * 2 + core, lax.rem(y, 2) * 4 + z)


def remote(src, dst, send, recv, where):
    return pltpu.make_async_remote_copy(
        src_ref=src, dst_ref=dst, send_sem=send, recv_sem=recv, device_id=where, device_id_type=MESH
    )


def greet(devices):
    barrier = pltpu.get_barrier_semaphore()
    for where in devices:
        pl.semaphore_signal(barrier, inc=1, device_id=where, device_id_type=MESH)
    pl.semaphore_wait(barrier, len(devices))


def exchange_kernel(
    meta_i, meta_w, edges, grid, teacher,
    sums, halo_lon, halo_lat, corner,
    mi_buf, mw_buf, mi_smem, mw_smem, relay_y, send, relay_x,
    sem_m, sem_ms, sem_h, sem_own, sem_core, sem_h1, sem_h2, sem_x1, sem_x2, sem_x3, sem_x0, *raw,
):
    x, y, z, core = my_place()
    other = 1 - core
    lon = lax.axis_index("lon")
    lat = lax.axis_index("lat")
    lon_up, lon_dn = lax.rem(lon + 1, 16), lax.rem(lon + 15, 16)
    lat_up, lat_dn = lax.rem(lat + 1, 8), lax.rem(lat + 7, 8)

    def sgn(way):
        return 1 if way == 0 else -1

    greet(
        [device(x, y, z, other)]
        + [device(x, y + s, z, h) for s in (1, -1) for h in (0, 1)]
        + [device(x + s, y, z, h) for s in (1, 2, 3) for h in (0, 1)]
        + [(lon_up, lat), (lon_dn, lat), (lon, lat_up), (lon, lat_dn)]
        + [(lon_up, lat_up), (lon_up, lat_dn), (lon_dn, lat_up), (lon_dn, lat_dn)]
    )

    def rows(half, ch):
        return pl.ds(pl.multiple_of(half * 128 + ch * CR, CR), CR)

    hop1, hop2, own, cross, fwd_x, all_x = {}, {}, {}, {}, {}, []

    def start_hop1(ch):
        for way in (0, 1):
            for h in (0, 1):
                copy = remote(
                    teacher.at[0, way * 4 : way * 4 + 4, rows(h, ch), :],
                    relay_y.at[ch, way, pl.ds(core * 4, 4)],
                    sem_h1.at[0, ch, way, h],
                    sem_h1.at[1, ch, way, core],
                    device(x, y + sgn(way), z, h),
                )
                copy.start()
                hop1[ch, way, h] = copy

    def arrived_hop1(ch, way, src_core):
        return remote(
            teacher.at[0, way * 4 : way * 4 + 4, rows(0, ch), :],
            relay_y.at[ch, way, src_core * 4 : src_core * 4 + 4],
            sem_h1.at[0, ch, way, src_core],
            sem_h1.at[1, ch, way, src_core],
            device(x, y - sgn(way), z, src_core),
        )

    def start_hop2(ch):
        for way in (0, 1):
            for src_core in (0, 1):
                arrived_hop1(ch, way, src_core).wait_recv()
            copy = remote(
                relay_y.at[ch, way],
                raw[ch].at[16 + way * 8 : 24 + way * 8],
                sem_h2.at[0, ch, way],
                sem_h2.at[1, ch, way],
                device(x, y + sgn(way), z, core),
            )
            copy.start()
            hop2[ch, way] = copy

    start_hop1(0)

    metas = []
    for d in (1, 2, 3, 0):
        for c in (0, 1):
            if d == 0 and c == 1:
                continue
            where = device(x + d, y, z, c if d else other)
            for kind, (src, dst) in enumerate(((meta_i, mi_buf), (meta_w, mw_buf))):
                tag = core if d else 0
                copy = remote(
                    src,
                    dst.at[(4 - d) % 4, core],
                    sem_m.at[0, kind, d, c],
                    sem_m.at[1, kind, (4 - d) % 4, tag],
                    where,
                )
                copy.start()
                metas.append(copy)
    mi_buf[0, core] = meta_i[...]
    mw_buf[0, core] = meta_w[...]

    for ch in range(NCH):
        copy = pltpu.make_async_copy(
            teacher.at[0, :, rows(core, ch), :], raw[ch].at[pl.ds(core * 8, 8)], sem_own.at[ch]
        )
        copy.start()
        own[ch] = copy
        copy = remote(
            teacher.at[0, :, rows(other, ch), :],
            raw[ch].at[pl.ds(core * 8, 8)],
            sem_core.at[0, ch],
            sem_core.at[1, ch],
            device(x, y, z, other),
        )
        copy.start()
        cross[ch] = copy

    if NCH > 1:
        start_hop1(1)

    halos = []
    for n, (src, dst, where) in enumerate(
        (
            (grid.at[63], halo_lon.at[0], (lon_up, lat)),
            (grid.at[0], halo_lon.at[1], (lon_dn, lat)),
            (edges.at[1], halo_lat.at[0], (lon, lat_up)),
            (edges.at[0], halo_lat.at[1], (lon, lat_dn)),
            (edges.at[1, 48:64], corner.at[0], (lon_up, lat_up)),
            (edges.at[0, 48:64], corner.at[1], (lon_up, lat_dn)),
            (edges.at[1, 0:16], corner.at[2], (lon_dn, lat_up)),
            (edges.at[0, 0:16], corner.at[3], (lon_dn, lat_dn)),
        )
    ):
        copy = remote(src, dst, sem_h.at[0, n], sem_h.at[1, n], where)
        copy.start()
        halos.append(copy)

    for s in range(4):
        for c in (0, 1):
            if s == 0 and c == 1:
                continue
            for kind, (src, dst) in enumerate(((meta_i, mi_buf), (meta_w, mw_buf))):
                remote(
                    src, dst.at[s, c if s else other],
                    sem_m.at[0, kind, s, c], sem_m.at[1, kind, s, c], device(x + s, y, z, c),
                ).wait_recv()
    to_smem = [
        pltpu.make_async_copy(mi_buf, mi_smem, sem_ms.at[0]),
        pltpu.make_async_copy(mw_buf, mw_smem, sem_ms.at[1]),
    ]
    for copy in to_smem:
        copy.start()
    for copy in to_smem:
        copy.wait()

    def pick(d, c, t, k):
        g = mi_smem[d, c, 0, t * 2 + k]
        w = mw_smem[d, c, 0, t * 2 + k]
        owner, block = g // 8, g % 8
        o_core, o_x, o_yhi = owner % 2, (owner // 2) % 4, owner // 8
        near = o_core * 8 + block
        far = 16 + (block // 4) * 8 + o_core * 4 + block % 4
        where = jnp.where(o_yhi == y // 2, near, far)
        return where, jnp.where(o_x == x, w, 0.0)

    def compute(ch):
        own[ch].wait()
        cross[ch].wait_recv()
        for way in (0, 1):
            hop2[ch, way].wait_recv()
        for d in range(4):

            def one(n, carry, d=d):
                if d == 2:
                    c, t = (n // 2) % 2, (n // 4) * 2 + n % 2
                else:
                    c, t = n // 4, n % 4
                i0, w0 = pick(d, c, t, 0)
                i1, w1 = pick(d, c, t, 1)
                total = w0 * raw[ch][i0].astype(F32) + w1 * raw[ch][i1].astype(F32)
                send[ch, d * 8 + n] = total.astype(BF16)
                return carry

            lax.fori_loop(0, 8, one, 0)

    def go(copy):
        copy.start()
        all_x.append(copy)

    def start_x(ch):
        for way, d in ((0, 2), (1, 2)):
            copy = remote(
                send.at[ch, 16 + way * 4 : 20 + way * 4],
                relay_x.at[ch, way],
                sem_x2.at[0, ch, way],
                sem_x2.at[1, ch, way],
                device(x + sgn(way), y, z, core),
            )
            copy.start()
            fwd_x[ch, way] = copy
        for d in (1, 3):
            for c in (0, 1):
                go(
                    remote(
                        send.at[ch, d * 8 + c * 4 : d * 8 + c * 4 + 4],
                        sums.at[4 - d, :, rows(core, ch), :],
                        sem_x1.at[0, ch, d // 2, c],
                        sem_x1.at[1, ch, d // 2, core],
                        device(x + d, y, z, c),
                    )
                )
        go(
            remote(
                send.at[ch, pl.ds(other * 4, 4)],
                sums.at[0, :, rows(core, ch), :],
                sem_x0.at[0, ch],
                sem_x0.at[1, ch],
                device(x, y, z, other),
            )
        )
        copy = pltpu.make_async_copy(
            send.at[ch, pl.ds(core * 4, 4)], sums.at[0, :, rows(core, ch), :], sem_x0.at[2, ch]
        )
        copy.start()
        own[ch, "x"] = copy

    def forward_x(ch):
        for way in (0, 1):
            fwd_x[ch, way].wait_recv()
            for c in (0, 1):
                go(
                    remote(
                        relay_x.at[ch, way, c * 2 : c * 2 + 2],
                        sums.at[2, way * 2 : way * 2 + 2, rows(core, ch), :],
                        sem_x3.at[0, ch, way, c],
                        sem_x3.at[1, ch, way, core],
                        device(x + sgn(way), y, z, c),
                    )
                )

    for ch in range(NCH):
        start_hop2(ch)
        if ch + 2 < NCH:
            start_hop1(ch + 2)
        if ch >= 1:
            compute(ch - 1)
            start_x(ch - 1)
        if ch >= 2:
            forward_x(ch - 2)
    compute(NCH - 1)
    start_x(NCH - 1)
    if NCH > 1:
        forward_x(NCH - 2)
    forward_x(NCH - 1)

    for copy in all_x:
        copy.wait_send()
    for ch in range(NCH):
        for d in (1, 3):
            for h in (0, 1):
                remote(
                    send.at[ch, 0:4],
                    sums.at[4 - d, :, rows(h, ch), :],
                    sem_x1.at[0, ch, d // 2, h],
                    sem_x1.at[1, ch, d // 2, h],
                    device(x + 1, y, z, h),
                ).wait_recv()
        remote(
            send.at[ch, 0:4],
            sums.at[0, :, rows(other, ch), :],
            sem_x0.at[0, ch],
            sem_x0.at[1, ch],
            device(x, y, z, other),
        ).wait_recv()
        own[ch, "x"].wait()
        for way in (0, 1):
            fwd_x[ch, way].wait_send()
            hop2[ch, way].wait_send()
            for h in (0, 1):
                hop1[ch, way, h].wait_send()
                remote(
                    relay_x.at[ch, way, 0:2],
                    sums.at[2, way * 2 : way * 2 + 2, rows(h, ch), :],
                    sem_x3.at[0, ch, way, h],
                    sem_x3.at[1, ch, way, h],
                    device(x + 1, y, z, h),
                ).wait_recv()
        cross[ch].wait_send()
    for copy in metas:
        copy.wait_send()
    for copy in halos:
        copy.wait()


def exchange(meta_i, meta_w, edges, grid, teacher):
    anywhere = pl.BlockSpec(memory_space=pl.ANY)
    vmem = pl.BlockSpec(memory_space=pltpu.VMEM)
    dma = pltpu.SemaphoreType.DMA
    return pl.pallas_call(
        exchange_kernel,
        out_shape=(
            jax.ShapeDtypeStruct((4, SLOTS, 256, C), BF16),
            jax.ShapeDtypeStruct((2, 32, C), BF16),
            jax.ShapeDtypeStruct((2, 64, C), BF16),
            jax.ShapeDtypeStruct((4, 16, C), BF16),
        ),
        in_specs=[vmem, vmem, anywhere, anywhere, anywhere],
        out_specs=(anywhere,) * 4,
        scratch_shapes=[
            pltpu.VMEM((4, 2, 8, 128), jnp.int32),
            pltpu.VMEM((4, 2, 8, 128), F32),
            pltpu.SMEM((4, 2, 8, 128), jnp.int32),
            pltpu.SMEM((4, 2, 8, 128), F32),
            pltpu.VMEM((NCH, 2, 8, CR, C), BF16),
            pltpu.VMEM((NCH, 32, CR, C), BF16),
            pltpu.VMEM((NCH, 2, 4, CR, C), BF16),
            dma((2, 2, 4, 2)),
            dma((2,)),
            dma((2, 8)),
            dma((NCH,)),
            dma((2, NCH)),
            dma((2, NCH, 2, 2)),
            dma((2, NCH, 2)),
            dma((2, NCH, 2, 2)),
            dma((2, NCH, 2)),
            dma((2, NCH, 2, 2)),
            dma((3, NCH)),
        ]
        + [pltpu.VMEM((32, CR, C), BF16)] * NCH,
        compiler_params=pltpu.CompilerParams(collective_id=0, has_side_effects=True),
    )(meta_i, meta_w, edges, grid, teacher)


def block_kernel(
    info, grid, halo_lon, halo_lat, corner, sums, conv, mix,
    next_ref, misfit_ref, own_ref, oth_ref,
    pad, lat_buf, cor_buf, xs, dp, hid, sc, grads, sem,
    *, scale,
):
    i = pl.program_id(0)
    core = info[16]
    low_ok, high_ok = info[17], info[18]

    @pl.when(i == 0)
    def _():
        copies = [
            pltpu.make_async_copy(grid, pad.at[1:65, 16:48], sem.at[0]),
            pltpu.make_async_copy(halo_lon.at[0], pad.at[0, 16:48], sem.at[1]),
            pltpu.make_async_copy(halo_lon.at[1], pad.at[65, 16:48], sem.at[2]),
            pltpu.make_async_copy(halo_lat, lat_buf, sem.at[3]),
            pltpu.make_async_copy(corner, cor_buf, sem.at[4]),
        ]
        for copy in copies:
            copy.start()
        xs[...] = jnp.zeros_like(xs)
        dp[...] = jnp.zeros_like(dp)
        hid[...] = jnp.zeros_like(hid)
        sc[...] = jnp.zeros_like(sc)
        for copy in copies:
            copy.wait()
        low = low_ok.astype(F32)
        high = high_ok.astype(F32)
        low_rows = (lat_buf[0].astype(F32) * low).reshape(64, 1, C)
        high_rows = (lat_buf[1].astype(F32) * high).reshape(64, 1, C)
        pad[1:65, 0:16] = jnp.broadcast_to(low_rows, (64, 16, C)).astype(BF16)
        pad[1:65, 48:64] = jnp.broadcast_to(high_rows, (64, 16, C)).astype(BF16)
        for n, (row, at, side, ok) in enumerate(
            ((15, 0, 0, low), (15, 0, 48, high), (0, 65, 0, low), (0, 65, 48, high))
        ):
            value = cor_buf[n].astype(F32)[row : row + 1] * ok
            pad[at, side : side + 16] = jnp.broadcast_to(value, (16, C)).astype(BF16)

    a, b = i // 2, i % 2
    ocean = info[i] == 1
    slot = info[8 + i]

    @pl.when(jnp.logical_not(ocean))
    def _():
        next_ref[...] = jnp.zeros_like(next_ref)
        misfit_ref[...] = jnp.zeros_like(misfit_ref)

    @pl.when(ocean)
    def _():
        def shift(line, carry):
            row = pad[a * 16 + line, pl.ds(pl.multiple_of(b * 16, 16), 48), :].astype(F32)
            at = pl.ds(pl.multiple_of(line * 16, 16), 16)
            xs[0, slot, at, :] = pltpu.roll(row, 1, 0)[16:32].astype(BF16)
            xs[1, slot, at, :] = row[16:32].astype(BF16)
            xs[2, slot, at, :] = pltpu.roll(row, 47, 0)[16:32].astype(BF16)
            return carry

        lax.fori_loop(0, 18, shift, 0)
        pre = jnp.zeros((256, C), F32)
        for tap in range(9):
            lon_step, lat_step = divmod(tap, 3)
            pre = pre + jnp.dot(
                xs[lat_step, slot, lon_step * 16 : lon_step * 16 + 256, :],
                conv[tap],
                preferred_element_type=F32,
            )
        sig = jax.nn.sigmoid(pre)
        hidden = (pre * sig).astype(BF16)
        full = xs[1, slot, 16:272, :].astype(F32) + jnp.dot(
            hidden, mix[...], preferred_element_type=F32
        )
        target = sums[0, slot].astype(F32)
        for n in range(1, 4):
            target = target + sums[n, slot].astype(F32)
        error = full - target
        next_ref[...] = full.astype(BF16).reshape(16, 16, C)
        misfit_ref[...] = error.astype(BF16).reshape(16, 16, C)
        scaled = (error * scale).astype(BF16)
        back = lax.dot_general(
            scaled, mix[...], (((1,), (1,)), ((), ())), preferred_element_type=F32
        )
        hid[slot] = hidden
        sc[slot] = scaled
        dp[slot] = (back * sig * (1.0 + pre * (1.0 - sig))).astype(BF16)

    @pl.when(i == pl.num_programs(0) - 1)
    def _():
        contract = (((0,), (0,)), ((), ()))
        dpre = dp[...].reshape(1024, C)
        for tap in range(9):
            lon_step, lat_step = divmod(tap, 3)
            grads[tap * C : (tap + 1) * C, :] = lax.dot_general(
                xs[lat_step, :, lon_step * 16 : lon_step * 16 + 256, :].reshape(1024, C),
                dpre,
                contract,
                preferred_element_type=F32,
            )
        grads[9 * C : 10 * C, :] = lax.dot_general(
            hid[...].reshape(1024, C), sc[...].reshape(1024, C), contract, preferred_element_type=F32
        )
        grads[10 * C : 2 * HALF, :] = jnp.zeros((2 * HALF - 10 * C, C), F32)

        def move(n, carry):
            at = pl.ds(pl.multiple_of(n * 64, 64), 64)
            own_ref[at, :] = grads[pl.ds(pl.multiple_of(core * HALF + n * 64, 64), 64), :]
            oth_ref[at, :] = grads[
                pl.ds(pl.multiple_of((1 - core) * HALF + n * 64, 64), 64), :
            ].astype(BF16)
            return carry

        lax.fori_loop(0, HALF // 64, move, 0)


def block(info, grid, halo_lon, halo_lat, corner, sums, conv, mix, scale):
    anywhere = pl.BlockSpec(memory_space=pl.ANY)
    vmem = pl.BlockSpec(memory_space=pltpu.VMEM)
    tile = pl.BlockSpec((TS, TS, C), lambda i, info: (i // 2, i % 2, 0))
    dma = pltpu.SemaphoreType.DMA
    return pl.pallas_call(
        functools.partial(block_kernel, scale=scale),
        out_shape=(
            jax.ShapeDtypeStruct((64, 32, C), BF16),
            jax.ShapeDtypeStruct((64, 32, C), BF16),
            jax.ShapeDtypeStruct((HALF, C), F32),
            jax.ShapeDtypeStruct((HALF, C), BF16),
        ),
        grid_spec=pltpu.PrefetchScalarGridSpec(
            num_scalar_prefetch=1,
            grid=(8,),
            in_specs=[anywhere] * 4 + [vmem] * 3,
            out_specs=(tile, tile, vmem, vmem),
            scratch_shapes=[
                pltpu.VMEM((66, 64, C), BF16),
                pltpu.VMEM((2, 64, C), BF16),
                pltpu.VMEM((4, 16, C), BF16),
                pltpu.VMEM((3, SLOTS, 288, C), BF16),
                pltpu.VMEM((SLOTS, 256, C), BF16),
                pltpu.VMEM((SLOTS, 256, C), BF16),
                pltpu.VMEM((SLOTS, 256, C), BF16),
                pltpu.VMEM((2 * HALF, C), F32),
                dma((5,)),
            ],
        ),
        compiler_params=pltpu.CompilerParams(
            dimension_semantics=("arbitrary",), vmem_limit_bytes=60 * 1024 * 1024
        ),
    )(info, grid, halo_lon, halo_lat, corner, sums, conv, mix)


def reduce_kernel(
    own, oth, out,
    rc, s1, r1, a1, r2, a2, r3, obuf,
    sem_c, sem_1, sem_2, sem_3, sem_g3, sem_g2, sem_g1, sem_gc, sem_o,
):
    x, y, z, core = my_place()
    place = (x, y, z)
    other = 1 - core

    def peer(dim, r):
        at = list(place)
        at[dim] = at[dim] + r
        return device(at[0], at[1], at[2], core)

    partner = device(x, y, z, other)
    greet([partner] + [peer(d, r) for d in range(3) for r in (1, 2, 3)])

    def col(q):
        return pl.ds(q * 128, 128)

    def at1(q, r):
        return pl.ds(pl.multiple_of(lax.rem(place[q] + r, 4) * 512, 512), 512)

    pend = []

    def go(copy):
        copy.start()
        pend.append(copy)
        return copy

    first = {}
    for r in (2, 1, 3, 0):
        for q in range(3):
            first[r, q] = go(
                remote(
                    oth.at[at1(q, r), col(q)], rc.at[at1(q, r), col(q)],
                    sem_c.at[0, r, q], sem_c.at[1, r, q], partner,
                )
            )
    one = {}
    for r in (2, 1, 3):
        for q in range(3):
            first[r, q].wait_recv()
            s1[r - 1, q] = (own[at1(q, r), col(q)] + rc[at1(q, r), col(q)].astype(F32)).astype(BF16)
            one[r, q] = go(
                remote(
                    s1.at[r - 1, q], r1.at[r - 1, q], sem_1.at[0, r - 1, q], sem_1.at[1, r - 1, q],
                    peer(q, r),
                )
            )
    for q in range(3):
        first[0, q].wait_recv()
        a1[q] = own[at1(q, 0), col(q)] + rc[at1(q, 0), col(q)].astype(F32)
    two = {}
    for q in range(3):
        for r in (1, 2, 3):
            one[r, q].wait_recv()
        a1[q] = a1[q] + (
            (r1[0, q].astype(F32) + r1[1, q].astype(F32)) + r1[2, q].astype(F32)
        )
        d1 = (q + 1) % 3
        for r in (2, 1, 3):
            v = lax.rem(place[d1] + r, 4)
            two[r, q] = go(
                remote(
                    a1.at[q, pl.ds(pl.multiple_of(v * 128, 128), 128)], r2.at[r - 1, q],
                    sem_2.at[0, r - 1, q], sem_2.at[1, r - 1, q], peer(d1, r),
                )
            )
    three = {}
    for q in range(3):
        d1, d2 = (q + 1) % 3, (q + 2) % 3
        for r in (1, 2, 3):
            two[r, q].wait_recv()
        mine = a1[q, pl.ds(pl.multiple_of(place[d1] * 128, 128), 128), :]
        a2[q] = mine + ((r2[0, q] + r2[1, q]) + r2[2, q])
        for r in (2, 1, 3):
            v = lax.rem(place[d2] + r, 4)
            three[r, q] = go(
                remote(
                    a2.at[q, pl.ds(pl.multiple_of(v * 32, 32), 32)], r3.at[r - 1, q],
                    sem_3.at[0, r - 1, q], sem_3.at[1, r - 1, q], peer(d2, r),
                )
            )
    base = core * HALF

    def span(q, level, shift=0):
        dims = (q, (q + 1) % 3, (q + 2) % 3)
        sizes = (512, 128, 32)
        start = base
        for n in range(level):
            v = place[dims[n]]
            if n == level - 1 and shift:
                v = lax.rem(v + shift, 4)
            start = start + v * sizes[n]
        size = sizes[level - 1]
        return obuf.at[pl.ds(pl.multiple_of(start, size), size), col(q)]

    def spread(q, level, sem):
        dim = (q + level - 1) % 3
        return {
            r: go(
                remote(
                    span(q, level), span(q, level), sem.at[0, r - 1, q], sem.at[1, r - 1, q], peer(dim, r)
                )
            )
            for r in (2, 1, 3)
        }

    g3, g2, g1, gc = {}, {}, {}, {}
    for q in range(3):
        d2 = (q + 2) % 3
        for r in (1, 2, 3):
            three[r, q].wait_recv()
        mine = a2[q, pl.ds(pl.multiple_of(place[d2] * 32, 32), 32), :]
        final = mine + ((r3[0, q] + r3[1, q]) + r3[2, q])
        start = base + place[q] * 512 + place[(q + 1) % 3] * 128 + place[d2] * 32
        obuf[pl.ds(pl.multiple_of(start, 32), 32), col(q)] = final.astype(BF16)
        g3[q] = spread(q, 3, sem_g3)
    for q in range(3):
        for r in (1, 2, 3):
            g3[q][r].wait_recv()
        g2[q] = spread(q, 2, sem_g2)

    def give(q, r):
        piece = span(q, 1, r)
        gc[q, r] = go(remote(piece, piece, sem_gc.at[0, r, q], sem_gc.at[1, r, q], partner))

    for q in range(3):
        for r in (1, 2, 3):
            g2[q][r].wait_recv()
        g1[q] = spread(q, 1, sem_g1)
        give(q, 0)
    for r in (1, 3, 2):
        for q in range(3):
            g1[q][r].wait_recv()
            give(q, 4 - r)
    for r in range(4):
        for q in range(3):
            gc[q, r].wait_recv()
    copy = pltpu.make_async_copy(obuf, out, sem_o.at[0])
    copy.start()
    for item in pend:
        item.wait_send()
    copy.wait()


def reduce(own, oth):
    anywhere = pl.BlockSpec(memory_space=pl.ANY)
    vmem = pl.BlockSpec(memory_space=pltpu.VMEM)
    dma = pltpu.SemaphoreType.DMA
    return pl.pallas_call(
        reduce_kernel,
        out_shape=jax.ShapeDtypeStruct((2 * HALF, C), BF16),
        in_specs=[vmem, anywhere],
        out_specs=anywhere,
        scratch_shapes=[
            pltpu.VMEM((HALF, C), BF16),
            pltpu.VMEM((3, 3, 512, 128), BF16),
            pltpu.VMEM((3, 3, 512, 128), BF16),
            pltpu.VMEM((3, 512, 128), F32),
            pltpu.VMEM((3, 3, 128, 128), F32),
            pltpu.VMEM((3, 128, 128), F32),
            pltpu.VMEM((3, 3, 32, 128), F32),
            pltpu.VMEM((2 * HALF, C), BF16),
            dma((2, 4, 3)),
            dma((2, 3, 3)),
            dma((2, 3, 3)),
            dma((2, 3, 3)),
            dma((2, 3, 3)),
            dma((2, 3, 3)),
            dma((2, 3, 3)),
            dma((2, 4, 3)),
            dma((1,)),
        ],
        compiler_params=pltpu.CompilerParams(collective_id=1, has_side_effects=True),
    )(own, oth)


def body(
    grid_state, conv_weight, mix_weight, teacher, tile_mask, source_owner, source_block, margin_weight
):
    lon = lax.axis_index("lon")
    lat = lax.axis_index("lat")
    lon_count = lax.axis_size("lon")
    lat_count = lax.axis_size("lat")
    width_lon, width_lat, chans = grid_state.shape
    scale = 1.0 / math.sqrt(width_lon * lon_count * width_lat * lat_count)
    ocean = tile_mask[0, 0]
    upto = jnp.arange(8)[:, None] <= jnp.arange(8)[None, :]
    rank = jnp.sum(jnp.where(upto, ocean[:, None], 0), axis=0) - 1
    chosen = (ocean[None, :] == 1) & (rank[None, :] == jnp.arange(SLOTS)[:, None])
    owner = lax.dynamic_index_in_dim(source_owner[0], lon, 0, keepdims=False)
    held = lax.dynamic_index_in_dim(source_block[0], lon, 0, keepdims=False)
    wanted = (owner * teacher.shape[1] + held).reshape(8, K)
    weight = margin_weight[0, 0].reshape(8, K)
    meta_i = jnp.sum(jnp.where(chosen[:, :, None], wanted[None], 0), axis=1).reshape(1, SLOTS * K)
    meta_w = jnp.sum(jnp.where(chosen[:, :, None], weight[None], 0.0), axis=1).reshape(1, SLOTS * K)
    meta_i = jnp.pad(meta_i, ((0, 7), (0, 128 - SLOTS * K)))
    meta_w = jnp.pad(meta_w, ((0, 7), (0, 128 - SLOTS * K)))
    edges = jnp.stack([grid_state[:, 0, :], grid_state[:, -1, :]])
    sums, halo_lon, halo_lat, corner = exchange(meta_i, meta_w, edges, grid_state, teacher)
    info = jnp.concatenate(
        [
            ocean,
            jnp.clip(rank, 0, SLOTS - 1),
            jnp.stack([lon % 2, (lat > 0).astype(jnp.int32), (lat < lat_count - 1).astype(jnp.int32)]),
        ]
    ).astype(jnp.int32)
    next_state, misfit, own, oth = block(
        info, grid_state, halo_lon, halo_lat, corner, sums, conv_weight, mix_weight, scale
    )
    total = reduce(own, oth)
    grad_conv = total[: 9 * chans].astype(F32).reshape(9, chans, chans)
    grad_mix = total[9 * chans : 10 * chans].astype(F32)
    return next_state, misfit, grad_conv, grad_mix


def solution(mesh):
    in_specs = (
        P("lon", "lat", None),
        P(),
        P(),
        P("lat", "lon", None, None),
        P("lon", "lat", None),
        P("lat", None, None),
        P("lat", None, None),
        P("lat", "lon", None),
    )
    out_specs = (P("lon", "lat", None), P("lon", "lat", None), P(), P())
    return jax.shard_map(body, mesh=mesh, in_specs=in_specs, out_specs=out_specs, check_vma=False)
```

time: 412 us -> 149 us (0.36); the launches traced: 407 us -> 149 us
  waiting for transfers between devices: 292 us -> 0 us
  Pallas kernels: 0 us -> 132 us
  matrix products: 51.4 us -> 0 us
  local copies, waits for them, and re-layouts: 28.7 us -> 6.67 us
  between operations: 14.9 us -> 0.69 us
  starting transfers between devices: 7.52 us -> 0 us
    psum x1 -> x0, waiting for transfers between devices: 155 us -> none  [body(): grad_conv, grad_mix = lax.psum((grad_conv, grad_mix), ('lon', 'lat'))]
    pallas_call x0 -> x3, Pallas kernels: none -> 132 us  [the longest x1 67.5 us: exchange(): pl.pallas_call(exchange_kernel, out_shape=(jax.ShapeDtypeStruct((4, SLOTS...]
    all_gather x1 -> x0, waiting for transfers between devices: 130 us -> none  [body(): piece = lax.all_gather(local_blocks, 'lon', axis=0, tiled=True)]
    dot_general x22 -> x0, matrix products: 51.4 us -> none  [the longest x9 16.4 us: block_step(): lax.dot_general(shifted(offset), dpre, (((0,), (0,)), ((), ())), preferre...]
    unnamed x55 -> x1, local copies, waits for them, and re-layouts: 13.8 us -> 0.51 us
    reduce_sum x1 -> x3, other arithmetic: 10.3 us -> 0.98 us  [the longest x1 0.74 us: body(): rank = jnp.sum(jnp.where(upto, ocean[:, None], 0), axis=0) - 1]
    reshape x1 -> x2, local copies, waits for them, and re-layouts: 8.16 us -> 0.17 us  [the longest x1 0.09 us: body(): jnp.sum(jnp.where(chosen[:, :, None], wanted[None], 0), axis=1)]
    ppermute x4 -> x0, waiting for transfers between devices: 7.64 us -> none  [the longest x2 4.4 us: with_halo(): lax.ppermute(tail, axis, [(i, (i + 1) % count) for i in range(ends)])]
  transfers between devices with their start and end apart: 6 -> 0, of which waited for: 4 -> 0; matrix products, arithmetic and copies ran while one was open for 6% -> 0% of each run, Pallas kernels for 0% -> 0%
where the time goes in v1:
time: 149 us
  Pallas kernels  132 us (89%)
  other arithmetic  8.97 us (6%)
  local copies, waits for them, and re-layouts  6.67 us (4%)
    pallas_call x1, Pallas kernels, exchange(): pl.pallas_call(exchange_kernel, out_shape=(jax.ShapeDtypeStruct((4, SLOTS...  67.5 us
    pallas_call x1, Pallas kernels, reduce(): pl.pallas_call(reduce_kernel, out_shape=jax.ShapeDtypeStruct((2 * HALF, C...  42.5 us
    pallas_call x1, Pallas kernels, block(): pl.pallas_call(functools.partial(block_kernel, scale=scale), out_shape=(j...  22.5 us

profile of v1, /device:TPU:1, one launch (start us, length us, event | category | flops | bytes accessed | tf_op | source)
XLA Modules:
  0.0 148.8 jit_solution(11054671300858260250)
XLA Ops:
  0.6 0.5 broadcast.61
  1.2 1.3 reduce.7
  2.5 0.7 add_reduce_fusion
  3.2 0.7 select_reduce_fusion.2
  3.9 0.7 broadcast_compare_fusion
  4.6 1.2 concatenate.3.info
  5.8 0.1 add.31
  5.9 0.1 copy.16
  6.0 0.1 select_reduce_fusion.1
  6.1 0.1 copy.17
  6.2 0.1 reshape.81
  6.3 0.6 pad.8.meta_i
  6.9 0.1 broadcast_in_dim.63
  7.0 0.1 copy.18
  7.1 0.1 select_reduce_fusion
  7.2 0.1 copy.19
  7.3 0.1 reshape.82
  7.4 0.6 pad.9.meta_w
  8.0 1.3 fusion.1
  9.3 0.7 pad_maximum_fusion.edges
  9.9 67.5 %shard_map.111 = (bf16[4,4,256,384]{3,2,1,0:T(8,128)(2,1)}, bf16[2,32,384]{2,1,0:T(8,128)(2,1)}, bf16[2,64,384]{2,1,0:T(8,128)(2,1)}, bf16[4,16,384]{2,1,0:T(8,128)(2,1)}) custom-call(s32[8,128]{1,0:T(8,128)} %pad.8.meta_i, f32[8,128]{1,0:T(8,128)} %pad.9.meta_w, bf16[2,64,384]{2,1,0:T(8,128)(2,1)} %pad_maximum_fusion.edges, bf16[64,32,384]{2,1,0:T(8,128)(2,1)} %grid.3, ...), custom_call_target="tpu_custom_call" | custom-call | tf_op jit(solution)/shard_map/pallas_call | solution.py:338
  77.4 22.5 %shard_map.112 = (bf16[64,32,384]{2,1,0:T(8,128)(2,1)}, bf16[64,32,384]{2,1,0:T(8,128)(2,1)}, f32[2048,384]{1,0:T(8,128)}, bf16[2048,384]{1,0:T(8,128)(2,1)}) custom-call(s32[19]{0:T(128)} %concatenate.3.info, bf16[64,32,384]{2,1,0:T(8,128)(2,1)} %grid.3, bf16[2,32,384]{2,1,0:T(8,128)(2,1)} %get-tuple-element.12.halo_lon, ...), custom_call_target="tpu_custom_call" | custom-call | tf_op jit(solution)/shard_map/pallas_call | solution.py:492
  100.0 42.5 %shard_map.113 = bf16[4096,384]{1,0:T(8,128)(2,1)} custom-call(f32[2048,384]{1,0:T(8,128)} %get-tuple-element.18.own, bf16[2048,384]{1,0:T(8,128)(2,1)} %get-tuple-element.19.oth), custom_call_target="tpu_custom_call" | custom-call | tf_op jit(solution)/shard_map/pallas_call | solution.py:674
  142.4 1.8 %slice_convert_fusion = f32[384,384]{1,0:T(8,128)} fusion(bf16[4096,384]{1,0:T(8,128)(2,1)} %shard_map.113), kind=kLoop, calls=%fused_computation | loop fusion | flops 147456 | bytes 884736 | tf_op jit(solution)/shard_map/convert_element_type | solution.py:737
  144.2 0.0 slice-start
  144.2 1.7 %slice-done = bf16[3456,384]{1,0:T(8,128)(2,1)S(1)} async-done(((bf16[4096,384]{1,0:T(8,128)(2,1)}), bf16[3456,384]{1,0:T(8,128)(2,1)S(1)}, s32[]{:S(2)}) %slice-start) | async-done | bytes 2654232 | tf_op jit(solution)/shard_map/slice | solution.py:736
  146.0 2.8 %convert.3 = f32[9,384,384]{2,1,0:T(8,128)} convert(bf16[9,384,384]{2,1,0:T(8,128)(2,1)S(1)} %bitcast.11) | non-fusion elementwise | flops 1327104 | bytes 7962624 | tf_op jit(solution)/shard_map/reshape | solution.py:736
  (3 shorter events, 0.0 us)
Async XLA Ops:
  144.2 1.7 %slice-start = ((bf16[4096,384]{1,0:T(8,128)(2,1)}), bf16[3456,384]{1,0:T(8,128)(2,1)S(1)}, s32[]{:S(2)}) async-start(bf16[4096,384]{1,0:T(8,128)(2,1)} %shard_map.113), calls=%async_computation | async-start | bytes 5308416 | tf_op jit(solution)/shard_map/slice | solution.py:736

commit v2 on v0

v2 whole, which is shorter than its diff:
```python
import functools
import math

import jax
import jax.numpy as jnp
from jax import lax
from jax.experimental import pallas as pl
from jax.experimental.pallas import tpu as pltpu
from jax.sharding import PartitionSpec as P

TS = 16
K = 2
SLOTS = 4
C = 384
NCH = 8
CR = 128 // NCH
HALF = 2048
MESH = pl.DeviceIdType.MESH
F32 = jnp.float32
BF16 = jnp.bfloat16


def my_place():
    lon = lax.axis_index("lon")
    lat = lax.axis_index("lat")
    core = lax.rem(lon, 2)
    x = lax.rem(lax.div(lon, 2), 4)
    y = lax.div(lon, 8) * 2 + lax.div(lat, 4)
    z = lax.rem(lat, 4)
    return x, y, z, core


def device(x, y, z, core):
    x = lax.rem(x + 8, 4)
    y = lax.rem(y + 8, 4)
    z = lax.rem(z + 8, 4)
    return (lax.div(y, 2) * 8 + x * 2 + core, lax.rem(y, 2) * 4 + z)


def remote(src, dst, send, recv, where):
    return pltpu.make_async_remote_copy(
        src_ref=src, dst_ref=dst, send_sem=send, recv_sem=recv, device_id=where, device_id_type=MESH
    )


def greet(devices):
    barrier = pltpu.get_barrier_semaphore()
    for where in devices:
        pl.semaphore_signal(barrier, inc=1, device_id=where, device_id_type=MESH)
    pl.semaphore_wait(barrier, len(devices))


def step_kernel(
    mask_ref, owner_ref, block_ref, margin_ref, grid, teacher, conv, mix,
    next_out, mis_out, conv_out, mix_out,
    mi_own, mw_own, mi_buf, mw_buf, mi_smem, mw_smem, send, sums,
    pad, lat_buf, cor_buf, edge, wbuf, mbuf, xs, pre_buf, full_buf, hid, sc, dp, next_buf, mis_buf,
    grads, gb, rc, s1, r1, a1, r2, a2, r3, obuf,
    sem_in, sem_m, sem_ms, sem_h, sem_own, sem_core, sem_far, sem_x1, sem_x0,
    sem_c, sem_1, sem_2, sem_3, sem_g3, sem_g2, sem_g1, sem_gc, sem_o, *raw,
    scale,
):
    x, y, z, core = my_place()
    place = (x, y, z)
    other = 1 - core
    lon = lax.axis_index("lon")
    lat = lax.axis_index("lat")
    lon_up, lon_dn = lax.rem(lon + 1, 16), lax.rem(lon + 15, 16)
    lat_up, lat_dn = lax.rem(lat + 1, 8), lax.rem(lat + 7, 8)
    partner = device(x, y, z, other)

    def peer(dim, r):
        at = list(place)
        at[dim] = at[dim] + r
        return device(at[0], at[1], at[2], core)

    loads = [
        pltpu.make_async_copy(grid, pad.at[1:65, 16:48], sem_in.at[0]),
        pltpu.make_async_copy(conv, wbuf, sem_in.at[1]),
        pltpu.make_async_copy(mix, mbuf, sem_in.at[2]),
    ]
    for copy in loads:
        copy.start()

    greet(
        [partner, device(x, y + 2, z, other)]
        + [peer(d, r) for d in range(3) for r in (1, 2, 3)]
        + [device(x + s, y, z, other) for s in (1, 2, 3)]
        + [(lon_up, lat), (lon_dn, lat), (lon, lat_up), (lon, lat_dn)]
        + [(lon_up, lat_up), (lon_up, lat_dn), (lon_dn, lat_up), (lon_dn, lat_dn)]
    )

    def rows(half, ch):
        return pl.ds(pl.multiple_of(half * 128 + ch * CR, CR), CR)

    far, own, cross, pend = {}, {}, {}, []

    def go(copy):
        copy.start()
        pend.append(copy)
        return copy

    def start_far(ch):
        for h in (0, 1):
            far[ch, h] = go(
                remote(
                    teacher.at[0, :, rows(h, ch), :],
                    raw[ch].at[pl.ds(16 + core * 8, 8)],
                    sem_far.at[0, ch, h],
                    sem_far.at[1, ch, core],
                    device(x, y + 2, z, h),
                )
            )

    def far_arrived(ch):
        for h in (0, 1):
            remote(
                teacher.at[0, :, rows(h, ch), :],
                raw[ch].at[16 + h * 8 : 24 + h * 8],
                sem_far.at[0, ch, h],
                sem_far.at[1, ch, h],
                device(x, y + 2, z, h),
            ).wait_recv()

    start_far(0)
    start_far(1)

    count = jnp.int32(0)
    chosen = []
    for i in range(8):
        on = mask_ref[0, 0, i]
        chosen.append([(on == 1) & (count == t) for t in range(SLOTS)])
        count = count + on
    lane = lax.broadcasted_iota(jnp.int32, (8, 128), 1)
    meta_i = jnp.zeros((8, 128), jnp.int32)
    meta_w = jnp.zeros((8, 128), F32)
    for k in range(K):
        wanted = [owner_ref[0, lon, i * K + k] * 8 + block_ref[0, lon, i * K + k] for i in range(8)]
        weight = [margin_ref[0, 0, i * K + k] for i in range(8)]
        for t in range(SLOTS):
            index, value = jnp.int32(0), jnp.float32(0)
            for i in range(8):
                index = jnp.where(chosen[i][t], wanted[i], index)
                value = jnp.where(chosen[i][t], weight[i], value)
            meta_i = jnp.where(lane == t * K + k, index, meta_i)
            meta_w = jnp.where(lane == t * K + k, value, meta_w)
    mi_own[...] = meta_i
    mw_own[...] = meta_w
    mi_buf[0, core] = meta_i
    mw_buf[0, core] = meta_w

    for d in (1, 2, 3, 0):
        for c in (0, 1):
            if d == 0 and c == 1:
                continue
            for kind, (src, dst) in enumerate(((mi_own, mi_buf), (mw_own, mw_buf))):
                go(
                    remote(
                        src,
                        dst.at[(4 - d) % 4, core],
                        sem_m.at[0, kind, d, c],
                        sem_m.at[1, kind, (4 - d) % 4, core if d else 0],
                        device(x + d, y, z, c if d else other),
                    )
                )

    for ch in range(NCH):
        copy = pltpu.make_async_copy(
            teacher.at[0, :, rows(core, ch), :], raw[ch].at[pl.ds(core * 8, 8)], sem_own.at[ch]
        )
        copy.start()
        own[ch] = copy
        cross[ch] = go(
            remote(
                teacher.at[0, :, rows(other, ch), :],
                raw[ch].at[pl.ds(core * 8, 8)],
                sem_core.at[0, ch],
                sem_core.at[1, ch],
                partner,
            )
        )
    start_far(2)

    loads[0].wait()
    spot = lax.broadcasted_iota(jnp.int32, (64, 1024), 1)
    line = lax.broadcasted_iota(jnp.int32, (64, 1024), 0) * 16
    for n, (side, at) in enumerate(((16, 0), (32, 15))):
        hot = (spot == line + at).astype(F32).astype(BF16)
        edge[n] = jnp.dot(
            hot, pad[1:65, side : side + 16].reshape(1024, C), preferred_element_type=F32
        ).astype(BF16)
    halos = []
    for n, (src, dst, where) in enumerate(
        (
            (grid.at[63], pad.at[0, 16:48], (lon_up, lat)),
            (grid.at[0], pad.at[65, 16:48], (lon_dn, lat)),
            (edge.at[1], lat_buf.at[0], (lon, lat_up)),
            (edge.at[0], lat_buf.at[1], (lon, lat_dn)),
            (edge.at[1, 48:64], cor_buf.at[0], (lon_up, lat_up)),
            (edge.at[0, 48:64], cor_buf.at[1], (lon_up, lat_dn)),
            (edge.at[1, 0:16], cor_buf.at[2], (lon_dn, lat_up)),
            (edge.at[0, 0:16], cor_buf.at[3], (lon_dn, lat_dn)),
        )
    ):
        halos.append(go(remote(src, dst, sem_h.at[0, n], sem_h.at[1, n], where)))
    for ch in range(3, NCH):
        start_far(ch)

    for s in range(4):
        for c in (0, 1):
            if s == 0 and c == 1:
                continue
            for kind, (src, dst) in enumerate(((mi_own, mi_buf), (mw_own, mw_buf))):
                remote(
                    src, dst.at[s, c if s else other],
                    sem_m.at[0, kind, s, c], sem_m.at[1, kind, s, c], device(x + s, y, z, c),
                ).wait_recv()
    to_smem = [
        pltpu.make_async_copy(mi_buf, mi_smem, sem_ms.at[0]),
        pltpu.make_async_copy(mw_buf, mw_smem, sem_ms.at[1]),
    ]
    for copy in to_smem:
        copy.start()
    for copy in halos:
        copy.wait_recv()
    low = (lat > 0).astype(F32)
    high = (lat < 7).astype(F32)
    low_rows = (lat_buf[0].astype(F32) * low).reshape(64, 1, C)
    high_rows = (lat_buf[1].astype(F32) * high).reshape(64, 1, C)
    pad[1:65, 0:16] = jnp.broadcast_to(low_rows, (64, 16, C)).astype(BF16)
    pad[1:65, 48:64] = jnp.broadcast_to(high_rows, (64, 16, C)).astype(BF16)
    for n, (row, at, side, ok) in enumerate(
        ((15, 0, 0, low), (15, 0, 48, high), (0, 65, 0, low), (0, 65, 48, high))
    ):
        value = cor_buf[n].astype(F32)[row : row + 1] * ok
        pad[at, side : side + 16] = jnp.broadcast_to(value, (16, C)).astype(BF16)
    for copy in to_smem:
        copy.wait()
    loads[1].wait()
    loads[2].wait()

    def pick(d, c, t, k):
        g = mi_smem[d, c, 0, t * 2 + k]
        w = mw_smem[d, c, 0, t * 2 + k]
        owner, block = g // 8, g % 8
        o_core, o_x, o_yhi = owner % 2, (owner // 2) % 4, owner // 8
        where = o_core * 8 + block + jnp.where(o_yhi == y // 2, 0, 16)
        return where, jnp.where(o_x == x, w, 0.0)

    def weigh(ch):
        own[ch].wait()
        cross[ch].wait_recv()
        far_arrived(ch)
        for d in range(4):

            def one(n, carry, d=d):
                c, t = n // 4, n % 4
                i0, w0 = pick(d, c, t, 0)
                i1, w1 = pick(d, c, t, 1)
                total = w0 * raw[ch][i0].astype(F32) + w1 * raw[ch][i1].astype(F32)
                send[ch, d * 8 + n] = total.astype(BF16)
                return carry

            lax.fori_loop(0, 8, one, 0)

    def start_x(ch):
        for d in (2, 1, 3):
            for c in (0, 1):
                go(
                    remote(
                        send.at[ch, d * 8 + c * 4 : d * 8 + c * 4 + 4],
                        sums.at[4 - d, :, rows(core, ch), :],
                        sem_x1.at[0, ch, d - 1, c],
                        sem_x1.at[1, ch, d - 1, core],
                        device(x + d, y, z, c),
                    )
                )
        go(
            remote(
                send.at[ch, pl.ds(other * 4, 4)],
                sums.at[0, :, rows(core, ch), :],
                sem_x0.at[0, ch],
                sem_x0.at[1, ch],
                partner,
            )
        )
        copy = pltpu.make_async_copy(
            send.at[ch, pl.ds(core * 4, 4)], sums.at[0, :, rows(core, ch), :], sem_x0.at[2, ch]
        )
        copy.start()
        own[ch, "x"] = copy

    tiles = []
    for t in range(SLOTS):
        tile = jnp.int32(0)
        for i in range(8):
            tile = jnp.where(chosen[i][t], i, tile)
        tiles.append(tile)

    def shift(m, carry):
        tile, n = m // 18, m % 18
        a, b = tile // 2, tile % 2
        row = pad[a * 16 + n, pl.ds(pl.multiple_of(b * 16, 16), 48), :].astype(F32)
        at = pl.ds(pl.multiple_of(n * 16, 16), 16)
        xs[0, tile, at, :] = pltpu.roll(row, 1, 0)[16:32].astype(BF16)
        xs[1, tile, at, :] = row[16:32].astype(BF16)
        xs[2, tile, at, :] = pltpu.roll(row, 47, 0)[16:32].astype(BF16)
        return carry

    def forward(t):
        pre = jnp.zeros((256, C), F32)
        for tap in range(9):
            lon_step, lat_step = divmod(tap, 3)
            pre = pre + jnp.dot(
                xs[lat_step, tiles[t], lon_step * 16 : lon_step * 16 + 256, :],
                wbuf[tap],
                preferred_element_type=F32,
            )
        hidden = (pre * jax.nn.sigmoid(pre)).astype(BF16)
        pre_buf[t] = pre
        hid[t] = hidden
        full = xs[1, tiles[t], 16:272, :].astype(F32) + jnp.dot(
            hidden, mbuf[...], preferred_element_type=F32
        )
        full_buf[t] = full
        next_buf[t] = full.astype(BF16)

    lax.fori_loop(0, 144, shift, 0)
    for ch in range(NCH):
        weigh(ch)
        start_x(ch)
        if ch < SLOTS:
            forward(ch)

    for ch in range(NCH):
        for h in (0, 1):
            for d in (1, 2, 3):
                remote(
                    send.at[ch, 0:4],
                    sums.at[4 - d, :, rows(h, ch), :],
                    sem_x1.at[0, ch, d - 1, h],
                    sem_x1.at[1, ch, d - 1, h],
                    device(x + 1, y, z, h),
                ).wait_recv()
        remote(
            send.at[ch, 0:4],
            sums.at[0, :, rows(other, ch), :],
            sem_x0.at[0, ch],
            sem_x0.at[1, ch],
            partner,
        ).wait_recv()
        own[ch, "x"].wait()

    def backward(t, carry):
        pre = pre_buf[t]
        sig = jax.nn.sigmoid(pre)
        target = sums[0, t].astype(F32)
        for n in range(1, 4):
            target = target + sums[n, t].astype(F32)
        error = (full_buf[t] - target) * (t < count).astype(F32)
        mis_buf[t] = error.astype(BF16)
        scaled = (error * scale).astype(BF16)
        back = lax.dot_general(
            scaled, mbuf[...], (((1,), (1,)), ((), ())), preferred_element_type=F32
        )
        sc[t] = scaled
        dp[t] = (back * sig * (1.0 + pre * (1.0 - sig))).astype(BF16)
        return carry

    lax.fori_loop(0, SLOTS, backward, 0)
    outs = [
        pltpu.make_async_copy(next_buf, next_out, sem_o.at[0]),
        pltpu.make_async_copy(mis_buf, mis_out, sem_o.at[1]),
    ]
    for copy in outs:
        copy.start()

    contract = (((0,), (0,)), ((), ()))
    for tap in range(10):
        lon_step, lat_step = divmod(tap, 3)
        if tap < 9:
            left = jnp.concatenate(
                [xs[lat_step, tile, lon_step * 16 : lon_step * 16 + 256, :] for tile in tiles]
            )
            right = dp[...].reshape(1024, C)
        else:
            left, right = hid[...].reshape(1024, C), sc[...].reshape(1024, C)
        grad = lax.dot_general(left, right, contract, preferred_element_type=F32)
        grads[tap * C : (tap + 1) * C, :] = grad
        gb[tap * C : (tap + 1) * C, :] = grad.astype(BF16)
    grads[10 * C : 2 * HALF, :] = jnp.zeros((2 * HALF - 10 * C, C), F32)
    gb[10 * C : 2 * HALF, :] = jnp.zeros((2 * HALF - 10 * C, C), BF16)

    def col(q):
        return pl.ds(q * 128, 128)

    def at1(q, r, half=None):
        start = lax.rem(place[q] + r, 4) * 512
        if half is not None:
            start = start + half * HALF
        return pl.ds(pl.multiple_of(start, 512), 512)

    first = {}
    for r in (2, 1, 3, 0):
        for q in range(3):
            first[r, q] = go(
                remote(
                    gb.at[at1(q, r, other), col(q)], rc.at[at1(q, r), col(q)],
                    sem_c.at[0, r, q], sem_c.at[1, r, q], partner,
                )
            )
    one = {}
    for r in (2, 1, 3):
        for q in range(3):
            first[r, q].wait_recv()
            s1[r - 1, q] = (grads[at1(q, r, core), col(q)] + rc[at1(q, r), col(q)].astype(F32)).astype(BF16)
            one[r, q] = go(
                remote(
                    s1.at[r - 1, q], r1.at[r - 1, q], sem_1.at[0, r - 1, q], sem_1.at[1, r - 1, q],
                    peer(q, r),
                )
            )
    for q in range(3):
        first[0, q].wait_recv()
        a1[q] = grads[at1(q, 0, core), col(q)] + rc[at1(q, 0), col(q)].astype(F32)
    two = {}
    for q in range(3):
        for r in (1, 2, 3):
            one[r, q].wait_recv()
        a1[q] = a1[q] + (
            (r1[0, q].astype(F32) + r1[1, q].astype(F32)) + r1[2, q].astype(F32)
        )
        d1 = (q + 1) % 3
        for r in (2, 1, 3):
            v = lax.rem(place[d1] + r, 4)
            two[r, q] = go(
                remote(
                    a1.at[q, pl.ds(pl.multiple_of(v * 128, 128), 128)], r2.at[r - 1, q],
                    sem_2.at[0, r - 1, q], sem_2.at[1, r - 1, q], peer(d1, r),
                )
            )
    three = {}
    for q in range(3):
        d1, d2 = (q + 1) % 3, (q + 2) % 3
        for r in (1, 2, 3):
            two[r, q].wait_recv()
        mine = a1[q, pl.ds(pl.multiple_of(place[d1] * 128, 128), 128), :]
        a2[q] = mine + ((r2[0, q] + r2[1, q]) + r2[2, q])
        for r in (2, 1, 3):
            v = lax.rem(place[d2] + r, 4)
            three[r, q] = go(
                remote(
                    a2.at[q, pl.ds(pl.multiple_of(v * 32, 32), 32)], r3.at[r - 1, q],
                    sem_3.at[0, r - 1, q], sem_3.at[1, r - 1, q], peer(d2, r),
                )
            )
    base = core * HALF

    def span(q, level, shift=0):
        dims = (q, (q + 1) % 3, (q + 2) % 3)
        sizes = (512, 128, 32)
        start = base
        for n in range(level):
            v = place[dims[n]]
            if n == level - 1 and shift:
                v = lax.rem(v + shift, 4)
            start = start + v * sizes[n]
        size = sizes[level - 1]
        return obuf.at[pl.ds(pl.multiple_of(start, size), size), col(q)]

    def spread(q, level, sem):
        dim = (q + level - 1) % 3
        return {
            r: go(
                remote(
                    span(q, level), span(q, level), sem.at[0, r - 1, q], sem.at[1, r - 1, q], peer(dim, r)
                )
            )
            for r in (2, 1, 3)
        }

    g3, g2, g1, gc = {}, {}, {}, {}
    for q in range(3):
        d2 = (q + 2) % 3
        for r in (1, 2, 3):
            three[r, q].wait_recv()
        mine = a2[q, pl.ds(pl.multiple_of(place[d2] * 32, 32), 32), :]
        final = mine + ((r3[0, q] + r3[1, q]) + r3[2, q])
        start = base + place[q] * 512 + place[(q + 1) % 3] * 128 + place[d2] * 32
        obuf[pl.ds(pl.multiple_of(start, 32), 32), col(q)] = final.astype(BF16)
        g3[q] = spread(q, 3, sem_g3)
    for q in range(3):
        for r in (1, 2, 3):
            g3[q][r].wait_recv()
        g2[q] = spread(q, 2, sem_g2)

    def give(q, r):
        piece = span(q, 1, r)
        gc[q, r] = go(remote(piece, piece, sem_gc.at[0, r, q], sem_gc.at[1, r, q], partner))

    for q in range(3):
        for r in (1, 2, 3):
            g2[q][r].wait_recv()
        g1[q] = spread(q, 1, sem_g1)
        give(q, 0)
    for r in (1, 3, 2):
        for q in range(3):
            g1[q][r].wait_recv()
            give(q, 4 - r)
    for r in range(4):
        for q in range(3):
            gc[q, r].wait_recv()
    outs += [
        pltpu.make_async_copy(obuf.at[0 : 9 * C], conv_out, sem_o.at[2]),
        pltpu.make_async_copy(obuf.at[9 * C : 10 * C], mix_out, sem_o.at[3]),
    ]
    for copy in outs[2:]:
        copy.start()
    for copy in pend:
        copy.wait_send()
    for copy in outs:
        copy.wait()


def step(tile_mask, source_owner, source_block, margin_weight, grid, teacher, conv, mix, scale):
    anywhere = pl.BlockSpec(memory_space=pl.ANY)
    smem = pl.BlockSpec(memory_space=pltpu.SMEM)
    dma = pltpu.SemaphoreType.DMA
    return pl.pallas_call(
        functools.partial(step_kernel, scale=scale),
        out_shape=(
            jax.ShapeDtypeStruct((SLOTS, 256, C), BF16),
            jax.ShapeDtypeStruct((SLOTS, 256, C), BF16),
            jax.ShapeDtypeStruct((9 * C, C), BF16),
            jax.ShapeDtypeStruct((C, C), BF16),
        ),
        in_specs=[smem] * 4 + [anywhere] * 4,
        out_specs=(anywhere,) * 4,
        scratch_shapes=[
            pltpu.VMEM((8, 128), jnp.int32),
            pltpu.VMEM((8, 128), F32),
            pltpu.VMEM((4, 2, 8, 128), jnp.int32),
            pltpu.VMEM((4, 2, 8, 128), F32),
            pltpu.SMEM((4, 2, 8, 128), jnp.int32),
            pltpu.SMEM((4, 2, 8, 128), F32),
            pltpu.VMEM((NCH, 32, CR, C), BF16),
            pltpu.VMEM((4, SLOTS, 256, C), BF16),
            pltpu.VMEM((66, 64, C), BF16),
            pltpu.VMEM((2, 64, C), BF16),
            pltpu.VMEM((4, 16, C), BF16),
            pltpu.VMEM((2, 64, C), BF16),
            pltpu.VMEM((9, C, C), BF16),
            pltpu.VMEM((C, C), BF16),
            pltpu.VMEM((3, 8, 288, C), BF16),
            pltpu.VMEM((SLOTS, 256, C), F32),
            pltpu.VMEM((SLOTS, 256, C), F32),
            pltpu.VMEM((SLOTS, 256, C), BF16),
            pltpu.VMEM((SLOTS, 256, C), BF16),
            pltpu.VMEM((SLOTS, 256, C), BF16),
            pltpu.VMEM((SLOTS, 256, C), BF16),
            pltpu.VMEM((SLOTS, 256, C), BF16),
            pltpu.VMEM((2 * HALF, C), F32),
            pltpu.VMEM((2 * HALF, C), BF16),
            pltpu.VMEM((HALF, C), BF16),
            pltpu.VMEM((3, 3, 512, 128), BF16),
            pltpu.VMEM((3, 3, 512, 128), BF16),
            pltpu.VMEM((3, 512, 128), F32),
            pltpu.VMEM((3, 3, 128, 128), F32),
            pltpu.VMEM((3, 128, 128), F32),
            pltpu.VMEM((3, 3, 32, 128), F32),
            pltpu.VMEM((2 * HALF, C), BF16),
            dma((3,)),
            dma((2, 2, 4, 2)),
            dma((2,)),
            dma((2, 8)),
            dma((NCH,)),
            dma((2, NCH)),
            dma((2, NCH, 2)),
            dma((2, NCH, 3, 2)),
            dma((3, NCH)),
            dma((2, 4, 3)),
            dma((2, 3, 3)),
            dma((2, 3, 3)),
            dma((2, 3, 3)),
            dma((2, 3, 3)),
            dma((2, 3, 3)),
            dma((2, 3, 3)),
            dma((2, 4, 3)),
            dma((4,)),
        ]
        + [pltpu.VMEM((32, CR, C), BF16)] * NCH,
        compiler_params=pltpu.CompilerParams(
            collective_id=0, has_side_effects=True, vmem_limit_bytes=60 * 1024 * 1024
        ),
    )(tile_mask, source_owner, source_block, margin_weight, grid, teacher, conv, mix)


def place_kernel(mask, next_in, mis_in, conv_in, mix_in, next_ref, mis_ref, conv_ref, mix_ref):
    i = pl.program_id(0)
    slot = jnp.int32(0)
    for j in range(8):
        slot = slot + jnp.where(j < i, mask[j], 0)
    slot = jnp.minimum(slot, SLOTS - 1)
    ocean = mask[i] == 1

    @pl.when(ocean)
    def _():
        next_ref[...] = next_in[slot].reshape(TS, TS, C)
        mis_ref[...] = mis_in[slot].reshape(TS, TS, C)

    @pl.when(jnp.logical_not(ocean))
    def _():
        next_ref[...] = jnp.zeros_like(next_ref)
        mis_ref[...] = jnp.zeros_like(mis_ref)

    conv_ref[...] = conv_in[...].astype(F32)
    mix_ref[...] = mix_in[...].astype(F32)


def place_tiles(mask, next_in, mis_in, conv_in, mix_in):
    tile = pl.BlockSpec((TS, TS, C), lambda i, mask: (i // 2, i % 2, 0))
    whole = pl.BlockSpec((SLOTS, 256, C), lambda i, mask: (0, 0, 0))
    conv = pl.BlockSpec((9 * C // 8, C), lambda i, mask: (i, 0))
    mix = pl.BlockSpec((C // 8, C), lambda i, mask: (i, 0))
    return pl.pallas_call(
        place_kernel,
        out_shape=(
            jax.ShapeDtypeStruct((64, 32, C), BF16),
            jax.ShapeDtypeStruct((64, 32, C), BF16),
            jax.ShapeDtypeStruct((9 * C, C), F32),
            jax.ShapeDtypeStruct((C, C), F32),
        ),
        grid_spec=pltpu.PrefetchScalarGridSpec(
            num_scalar_prefetch=1,
            grid=(8,),
            in_specs=[whole, whole, conv, mix],
            out_specs=(tile, tile, conv, mix),
        ),
        compiler_params=pltpu.CompilerParams(dimension_semantics=("arbitrary",)),
    )(mask, next_in, mis_in, conv_in, mix_in)


def body(
    grid_state, conv_weight, mix_weight, teacher, tile_mask, source_owner, source_block, margin_weight
):
    width_lon, width_lat, chans = grid_state.shape
    cells = width_lon * lax.axis_size("lon") * width_lat * lax.axis_size("lat")
    parts = step(
        tile_mask, source_owner, source_block, margin_weight, grid_state, teacher,
        conv_weight, mix_weight, 1.0 / math.sqrt(cells),
    )
    next_state, misfit, grad_conv, grad_mix = place_tiles(tile_mask.reshape(8), *parts)
    return next_state, misfit, grad_conv.reshape(9, chans, chans), grad_mix


def solution(mesh):
    in_specs = (
        P("lon", "lat", None),
        P(),
        P(),
        P("lat", "lon", None, None),
        P("lon", "lat", None),
        P("lat", None, None),
        P("lat", None, None),
        P("lat", "lon", None),
    )
    out_specs = (P("lon", "lat", None), P("lon", "lat", None), P(), P())
    return jax.shard_map(body, mesh=mesh, in_specs=in_specs, out_specs=out_specs, check_vma=False)
```

time: 412 us -> 125 us (0.30); the launches traced: 407 us -> 125 us
  waiting for transfers between devices: 292 us -> 0 us
  Pallas kernels: 0 us -> 124 us
  matrix products: 51.4 us -> 0 us
  local copies, waits for them, and re-layouts: 28.7 us -> 0 us
  between operations: 14.9 us -> 0.64 us
  other arithmetic: 12.3 us -> 0 us
  starting transfers between devices: 7.52 us -> 0 us
    psum x1 -> x0, waiting for transfers between devices: 155 us -> none  [body(): grad_conv, grad_mix = lax.psum((grad_conv, grad_mix), ('lon', 'lat'))]
    all_gather x1 -> x0, waiting for transfers between devices: 130 us -> none  [body(): piece = lax.all_gather(local_blocks, 'lon', axis=0, tiled=True)]
    pallas_call x0 -> x2, Pallas kernels: none -> 124 us  [the longest x1 116 us: step(): pl.pallas_call(functools.partial(step_kernel, scale=scale), out_shape=(ja...]
    dot_general x22 -> x0, matrix products: 51.4 us -> none  [the longest x9 16.4 us: block_step(): lax.dot_general(shifted(offset), dpre, (((0,), (0,)), ((), ())), preferre...]
    unnamed x55 -> x0, local copies, waits for them, and re-layouts: 13.8 us -> none
    reduce_sum x1 -> x0, other arithmetic: 10.3 us -> none  [body(): jnp.sum(mixed.reshape(tile_count, K, cells_tile, chans), axis=1)]
    reshape x1 -> x0, local copies, waits for them, and re-layouts: 8.16 us -> none  [body(): mixed.reshape(tile_count, K, cells_tile, chans)]
    ppermute x4 -> x0, waiting for transfers between devices: 7.64 us -> none  [the longest x2 4.4 us: with_halo(): lax.ppermute(tail, axis, [(i, (i + 1) % count) for i in range(ends)])]
  transfers between devices with their start and end apart: 6 -> 0, of which waited for: 4 -> 0; matrix products, arithmetic and copies ran while one was open for 6% -> 0% of each run, Pallas kernels for 0% -> 0%
where the time goes in v2:
time: 125 us
  Pallas kernels  124 us (99%)
    pallas_call x1, Pallas kernels, step(): pl.pallas_call(functools.partial(step_kernel, scale=scale), out_shape=(ja...  116 us
    pallas_call x1, Pallas kernels, place_tiles(): pl.pallas_call(place_kernel, out_shape=(jax.ShapeDtypeStruct((64, 32, C),...  8.34 us

profile of v2, /device:TPU:1, one launch (start us, length us, event | category | flops | bytes accessed | tf_op | source)
XLA Modules:
  0.0 124.9 jit_solution(4590638653021424542)
XLA Ops:
  0.6 115.9 %shard_map.111 = (bf16[4,256,384]{2,1,0:T(8,128)(2,1)}, bf16[4,256,384]{2,1,0:T(8,128)(2,1)}, bf16[3456,384]{1,0:T(8,128)(2,1)}, bf16[384,384]{1,0:T(8,128)(2,1)}) custom-call(s32[1,1,8]{2,1,0:T(1,128)} %mask_ref.1, s32[1,16,16]{2,1,0:T(8,128)} %owner_ref.1, s32[1,16,16]{2,1,0:T(8,128)} %block_ref.1, f32[1,1,16]{2,1,0:T(1,128)} %margin_ref.1, ...), custom_call_target="tpu_custom_call" | custom-call | tf_op jit(solution)/shard_map/pallas_call | solution.py:529
  116.5 8.3 %shard_map.112 = (bf16[64,32,384]{2,1,0:T(8,128)(2,1)}, bf16[64,32,384]{2,1,0:T(8,128)(2,1)}, f32[3456,384]{1,0:T(8,128)}, f32[384,384]{1,0:T(8,128)}) custom-call(s32[8]{0:T(128)} %bitcast.2, bf16[4,256,384]{2,1,0:T(8,128)(2,1)} %get-tuple-element.12.next_in, bf16[4,256,384]{2,1,0:T(8,128)(2,1)} %get-tuple-element.13.mis_in, ...), custom_call_target="tpu_custom_call" | custom-call | tf_op jit(solution)/shard_map/pallas_call | solution.py:625

commit v3 on v2

--- a/solution.py
+++ b/solution.py
@@ -15,6 +15,8 @@
 NCH = 8
 CR = 128 // NCH
 HALF = 2048
+SUBS = 2
+PIECE = HALF // (4 * SUBS)
 MESH = pl.DeviceIdType.MESH
 F32 = jnp.float32
 BF16 = jnp.bfloat16
@@ -87,7 +89,6 @@
         + [peer(d, r) for d in range(3) for r in (1, 2, 3)]
         + [device(x + s, y, z, other) for s in (1, 2, 3)]
         + [(lon_up, lat), (lon_dn, lat), (lon, lat_up), (lon, lat_dn)]
-        + [(lon_up, lat_up), (lon_up, lat_dn), (lon_dn, lat_up), (lon_dn, lat_dn)]
     )
 
     def rows(half, ch):
@@ -131,9 +132,9 @@
         on = mask_ref[0, 0, i]
         chosen.append([(on == 1) & (count == t) for t in range(SLOTS)])
         count = count + on
-    lane = lax.broadcasted_iota(jnp.int32, (8, 128), 1)
-    meta_i = jnp.zeros((8, 128), jnp.int32)
-    meta_w = jnp.zeros((8, 128), F32)
+    lane = lax.broadcasted_iota(jnp.int32, (1, 128), 1)
+    meta_i = jnp.zeros((1, 128), jnp.int32)
+    meta_w = jnp.zeros((1, 128), F32)
     for k in range(K):
         wanted = [owner_ref[0, lon, i * K + k] * 8 + block_ref[0, lon, i * K + k] for i in range(8)]
         weight = [margin_ref[0, 0, i * K + k] for i in range(8)]
@@ -196,16 +197,9 @@
             (grid.at[0], pad.at[65, 16:48], (lon_dn, lat)),
             (edge.at[1], lat_buf.at[0], (lon, lat_up)),
             (edge.at[0], lat_buf.at[1], (lon, lat_dn)),
-            (edge.at[1, 48:64], cor_buf.at[0], (lon_up, lat_up)),
-            (edge.at[0, 48:64], cor_buf.at[1], (lon_up, lat_dn)),
-            (edge.at[1, 0:16], cor_buf.at[2], (lon_dn, lat_up)),
-            (edge.at[0, 0:16], cor_buf.at[3], (lon_dn, lat_dn)),
         )
     ):
         halos.append(go(remote(src, dst, sem_h.at[0, n], sem_h.at[1, n], where)))
-    for ch in range(3, NCH):
-        start_far(ch)
-
     for s in range(4):
         for c in (0, 1):
             if s == 0 and c == 1:
@@ -221,23 +215,8 @@
     ]
     for copy in to_smem:
         copy.start()
-    for copy in halos:
-        copy.wait_recv()
-    low = (lat > 0).astype(F32)
-    high = (lat < 7).astype(F32)
-    low_rows = (lat_buf[0].astype(F32) * low).reshape(64, 1, C)
-    high_rows = (lat_buf[1].astype(F32) * high).reshape(64, 1, C)
-    pad[1:65, 0:16] = jnp.broadcast_to(low_rows, (64, 16, C)).astype(BF16)
-    pad[1:65, 48:64] = jnp.broadcast_to(high_rows, (64, 16, C)).astype(BF16)
-    for n, (row, at, side, ok) in enumerate(
-        ((15, 0, 0, low), (15, 0, 48, high), (0, 65, 0, low), (0, 65, 48, high))
-    ):
-        value = cor_buf[n].astype(F32)[row : row + 1] * ok
-        pad[at, side : side + 16] = jnp.broadcast_to(value, (16, C)).astype(BF16)
     for copy in to_smem:
         copy.wait()
-    loads[1].wait()
-    loads[2].wait()
 
     def pick(d, c, t, k):
         g = mi_smem[d, c, 0, t * 2 + k]
@@ -325,12 +304,50 @@
         full_buf[t] = full
         next_buf[t] = full.astype(BF16)
 
-    lax.fori_loop(0, 144, shift, 0)
+    def corners():
+        for copy in halos[2:4]:
+            copy.wait_recv()
+        for n, (src, where) in enumerate(
+            (
+                (lat_buf.at[0, 48:64], (lon_up, lat)),
+                (lat_buf.at[1, 48:64], (lon_up, lat)),
+                (lat_buf.at[0, 0:16], (lon_dn, lat)),
+                (lat_buf.at[1, 0:16], (lon_dn, lat)),
+            )
+        ):
+            halos.append(
+                go(remote(src, cor_buf.at[n], sem_h.at[0, 4 + n], sem_h.at[1, 4 + n], where))
+            )
+
+    def windows():
+        for copy in halos[:2] + halos[4:]:
+            copy.wait_recv()
+        low = (lat > 0).astype(F32)
+        high = (lat < 7).astype(F32)
+        low_rows = (lat_buf[0].astype(F32) * low).reshape(64, 1, C)
+        high_rows = (lat_buf[1].astype(F32) * high).reshape(64, 1, C)
+        pad[1:65, 0:16] = jnp.broadcast_to(low_rows, (64, 16, C)).astype(BF16)
+        pad[1:65, 48:64] = jnp.broadcast_to(high_rows, (64, 16, C)).astype(BF16)
+        for n, (row, at, side, ok) in enumerate(
+            ((15, 0, 0, low), (15, 0, 48, high), (0, 65, 0, low), (0, 65, 48, high))
+        ):
+            value = cor_buf[n].astype(F32)[row : row + 1] * ok
+            pad[at, side : side + 16] = jnp.broadcast_to(value, (16, C)).astype(BF16)
+        lax.fori_loop(0, 144, shift, 0)
+        loads[1].wait()
+        loads[2].wait()
+
     for ch in range(NCH):
         weigh(ch)
+        if ch + 3 < NCH:
+            start_far(ch + 3)
         start_x(ch)
-        if ch < SLOTS:
-            forward(ch)
+        if ch == 0:
+            corners()
+        elif ch == 1:
+            windows()
+        elif ch < SLOTS + 2:
+            forward(ch - 2)
 
     for ch in range(NCH):
         for h in (0, 1):
@@ -394,122 +411,124 @@
     def col(q):
         return pl.ds(q * 128, 128)
 
-    def at1(q, r, half=None):
-        start = lax.rem(place[q] + r, 4) * 512
+    def at1(p, r, half=None):
+        start = (p // 3) * (HALF // SUBS) + lax.rem(place[p % 3] + r, 4) * PIECE
         if half is not None:
             start = start + half * HALF
-        return pl.ds(pl.multiple_of(start, 512), 512)
-
-    first = {}
-    for r in (2, 1, 3, 0):
-        for q in range(3):
-            first[r, q] = go(
-                remote(
-                    gb.at[at1(q, r, other), col(q)], rc.at[at1(q, r), col(q)],
-                    sem_c.at[0, r, q], sem_c.at[1, r, q], partner,
+        return pl.ds(pl.multiple_of(start, PIECE), PIECE)
+
+    def dims(p):
+        return p % 3, (p + 1) % 3, (p + 2) % 3
+
+    groups = [range(3 * u, 3 * u + 3) for u in range(SUBS)]
+    parts = range(3 * SUBS)
+    sizes = (PIECE, PIECE // 4, PIECE // 16)
+    first, one, two, three, g3, g2, g1, gc = {}, {}, {}, {}, {}, {}, {}, {}
+    for group in groups:
+        for r in (2, 1, 3, 0):
+            for p in group:
+                first[r, p] = go(
+                    remote(
+                        gb.at[at1(p, r, other), col(p % 3)], rc.at[at1(p, r), col(p % 3)],
+                        sem_c.at[0, r, p], sem_c.at[1, r, p], partner,
+                    )
                 )
-            )
-    one = {}
-    for r in (2, 1, 3):
-        for q in range(3):
-            first[r, q].wait_recv()
-            s1[r - 1, q] = (grads[at1(q, r, core), col(q)] + rc[at1(q, r), col(q)].astype(F32)).astype(BF16)
-            one[r, q] = go(
-                remote(
-                    s1.at[r - 1, q], r1.at[r - 1, q], sem_1.at[0, r - 1, q], sem_1.at[1, r - 1, q],
-                    peer(q, r),
+    for group in groups:
+        for r in (2, 1, 3):
+            for p in group:
+                first[r, p].wait_recv()
+                s1[r - 1, p] = (
+                    grads[at1(p, r, core), col(p % 3)] + rc[at1(p, r), col(p % 3)].astype(F32)
+                ).astype(BF16)
+                one[r, p] = go(
+                    remote(
+                        s1.at[r - 1, p], r1.at[r - 1, p],
+                        sem_1.at[0, r - 1, p], sem_1.at[1, r - 1, p], peer(p % 3, r),
+                    )
                 )
-            )
-    for q in range(3):
-        first[0, q].wait_recv()
-        a1[q] = grads[at1(q, 0, core), col(q)] + rc[at1(q, 0), col(q)].astype(F32)
-    two = {}
-    for q in range(3):
+    for p in parts:
+        first[0, p].wait_recv()
+        a1[p] = grads[at1(p, 0, core), col(p % 3)] + rc[at1(p, 0), col(p % 3)].astype(F32)
+    for p in parts:
         for r in (1, 2, 3):
-            one[r, q].wait_recv()
-        a1[q] = a1[q] + (
-            (r1[0, q].astype(F32) + r1[1, q].astype(F32)) + r1[2, q].astype(F32)
+            one[r, p].wait_recv()
+        a1[p] = a1[p] + (
+            (r1[0, p].astype(F32) + r1[1, p].astype(F32)) + r1[2, p].astype(F32)
         )
-        d1 = (q + 1) % 3
+        d1 = dims(p)[1]
         for r in (2, 1, 3):
             v = lax.rem(place[d1] + r, 4)
-            two[r, q] = go(
+            two[r, p] = go(
                 remote(
-                    a1.at[q, pl.ds(pl.multiple_of(v * 128, 128), 128)], r2.at[r - 1, q],
-                    sem_2.at[0, r - 1, q], sem_2.at[1, r - 1, q], peer(d1, r),
+                    a1.at[p, pl.ds(pl.multiple_of(v * sizes[1], sizes[1]), sizes[1])],
+                    r2.at[r - 1, p],
+                    sem_2.at[0, r - 1, p], sem_2.at[1, r - 1, p], peer(d1, r),
                 )
             )
-    three = {}
-    for q in range(3):
-        d1, d2 = (q + 1) % 3, (q + 2) % 3
+    for p in parts:
+        _, d1, d2 = dims(p)
         for r in (1, 2, 3):
-            two[r, q].wait_recv()
-        mine = a1[q, pl.ds(pl.multiple_of(place[d1] * 128, 128), 128), :]
-        a2[q] = mine + ((r2[0, q] + r2[1, q]) + r2[2, q])
+            two[r, p].wait_recv()
+        mine = a1[p, pl.ds(pl.multiple_of(place[d1] * sizes[1], sizes[1]), sizes[1]), :]
+        a2[p] = mine + ((r2[0, p] + r2[1, p]) + r2[2, p])
         for r in (2, 1, 3):
             v = lax.rem(place[d2] + r, 4)
-            three[r, q] = go(
+            three[r, p] = go(
                 remote(
-                    a2.at[q, pl.ds(pl.multiple_of(v * 32, 32), 32)], r3.at[r - 1, q],
-                    sem_3.at[0, r - 1, q], sem_3.at[1, r - 1, q], peer(d2, r),
+                    a2.at[p, pl.ds(pl.multiple_of(v * sizes[2], sizes[2]), sizes[2])],
+                    r3.at[r - 1, p],
+                    sem_3.at[0, r - 1, p], sem_3.at[1, r - 1, p], peer(d2, r),
                 )
             )
-    base = core * HALF
-
-    def span(q, level, shift=0):
-        dims = (q, (q + 1) % 3, (q + 2) % 3)
-        sizes = (512, 128, 32)
-        start = base
+
+    def span(p, level, shift=0):
+        start = core * HALF + (p // 3) * (HALF // SUBS)
         for n in range(level):
-            v = place[dims[n]]
+            v = place[dims(p)[n]]
             if n == level - 1 and shift:
                 v = lax.rem(v + shift, 4)
             start = start + v * sizes[n]
         size = sizes[level - 1]
-        return obuf.at[pl.ds(pl.multiple_of(start, size), size), col(q)]
-
-    def spread(q, level, sem):
-        dim = (q + level - 1) % 3
+        return pl.ds(pl.multiple_of(start, size), size), col(p % 3)
+
+    def spread(p, level, sem):
+        dim = dims(p)[level - 1]
+        piece = obuf.at[span(p, level)]
         return {
-            r: go(
-                remote(
-                    span(q, level), span(q, level), sem.at[0, r - 1, q], sem.at[1, r - 1, q], peer(dim, r)
-                )
-            )
+            r: go(remote(piece, piece, sem.at[0, r - 1, p], sem.at[1, r - 1, p], peer(dim, r)))
             for r in (2, 1, 3)
         }
 
-    g3, g2, g1, gc = {}, {}, {}, {}
-    for q in range(3):
-        d2 = (q + 2) % 3
+    for p in parts:
+        d2 = dims(p)[2]
         for r in (1, 2, 3):
-            three[r, q].wait_recv()
-        mine = a2[q, pl.ds(pl.multiple_of(place[d2] * 32, 32), 32), :]
-        final = mine + ((r3[0, q] + r3[1, q]) + r3[2, q])
-        start = base + place[q] * 512 + place[(q + 1) % 3] * 128 + place[d2] * 32
-        obuf[pl.ds(pl.multiple_of(start, 32), 32), col(q)] = final.astype(BF16)
-        g3[q] = spread(q, 3, sem_g3)
-    for q in range(3):
+            three[r, p].wait_recv()
+        mine = a2[p, pl.ds(pl.multiple_of(place[d2] * sizes[2], sizes[2]), sizes[2]), :]
+        final = mine + ((r3[0, p] + r3[1, p]) + r3[2, p])
+        obuf[span(p, 3)] = final.astype(BF16)
+        g3[p] = spread(p, 3, sem_g3)
+    for p in parts:
         for r in (1, 2, 3):
-            g3[q][r].wait_recv()
-        g2[q] = spread(q, 2, sem_g2)
-
-    def give(q, r):
-        piece = span(q, 1, r)
-        gc[q, r] = go(remote(piece, piece, sem_gc.at[0, r, q], sem_gc.at[1, r, q], partner))
-
-    for q in range(3):
+            g3[p][r].wait_recv()
+        g2[p] = spread(p, 2, sem_g2)
+
+    def give(p, r):
+        piece = obuf.at[span(p, 1, r)]
+        gc[p, r] = go(remote(piece, piece, sem_gc.at[0, r, p], sem_gc.at[1, r, p], partner))
+
+    for p in parts:
         for r in (1, 2, 3):
-            g2[q][r].wait_recv()
-        g1[q] = spread(q, 1, sem_g1)
-        give(q, 0)
-    for r in (1, 3, 2):
-        for q in range(3):
-            g1[q][r].wait_recv()
-            give(q, 4 - r)
+            g2[p][r].wait_recv()
+        g1[p] = spread(p, 1, sem_g1)
+        give(p, 0)
+    for group in groups:
+        for r in (1, 3, 2):
+            for p in group:
+                g1[p][r].wait_recv()
+                give(p, 4 - r)
     for r in range(4):
-        for q in range(3):
-            gc[q, r].wait_recv()
+        for p in parts:
+            gc[p, r].wait_recv()
     outs += [
         pltpu.make_async_copy(obuf.at[0 : 9 * C], conv_out, sem_o.at[2]),
         pltpu.make_async_copy(obuf.at[9 * C : 10 * C], mix_out, sem_o.at[3]),
@@ -537,12 +556,12 @@
         in_specs=[smem] * 4 + [anywhere] * 4,
         out_specs=(anywhere,) * 4,
         scratch_shapes=[
-            pltpu.VMEM((8, 128), jnp.int32),
-            pltpu.VMEM((8, 128), F32),
-            pltpu.VMEM((4, 2, 8, 128), jnp.int32),
-            pltpu.VMEM((4, 2, 8, 128), F32),
-            pltpu.SMEM((4, 2, 8, 128), jnp.int32),
-            pltpu.SMEM((4, 2, 8, 128), F32),
+            pltpu.VMEM((1, 128), jnp.int32),
+            pltpu.VMEM((1, 128), F32),
+            pltpu.VMEM((4, 2, 1, 128), jnp.int32),
+            pltpu.VMEM((4, 2, 1, 128), F32),
+            pltpu.SMEM((4, 2, 1, 128), jnp.int32),
+            pltpu.SMEM((4, 2, 1, 128), F32),
             pltpu.VMEM((NCH, 32, CR, C), BF16),
             pltpu.VMEM((4, SLOTS, 256, C), BF16),
             pltpu.VMEM((66, 64, C), BF16),
@@ -562,12 +581,12 @@
             pltpu.VMEM((2 * HALF, C), F32),
             pltpu.VMEM((2 * HALF, C), BF16),
             pltpu.VMEM((HALF, C), BF16),
-            pltpu.VMEM((3, 3, 512, 128), BF16),
-            pltpu.VMEM((3, 3, 512, 128), BF16),
-            pltpu.VMEM((3, 512, 128), F32),
-            pltpu.VMEM((3, 3, 128, 128), F32),
-            pltpu.VMEM((3, 128, 128), F32),
-            pltpu.VMEM((3, 3, 32, 128), F32),
+            pltpu.VMEM((3, 3 * SUBS, PIECE, 128), BF16),
+            pltpu.VMEM((3, 3 * SUBS, PIECE, 128), BF16),
+            pltpu.VMEM((3 * SUBS, PIECE, 128), F32),
+            pltpu.VMEM((3, 3 * SUBS, PIECE // 4, 128), F32),
+            pltpu.VMEM((3 * SUBS, PIECE // 4, 128), F32),
+            pltpu.VMEM((3, 3 * SUBS, PIECE // 16, 128), F32),
             pltpu.VMEM((2 * HALF, C), BF16),
             dma((3,)),
             dma((2, 2, 4, 2)),
@@ -578,14 +597,14 @@
             dma((2, NCH, 2)),
             dma((2, NCH, 3, 2)),
             dma((3, NCH)),
-            dma((2, 4, 3)),
-            dma((2, 3, 3)),
-            dma((2, 3, 3)),
-            dma((2, 3, 3)),
-            dma((2, 3, 3)),
-            dma((2, 3, 3)),
-            dma((2, 3, 3)),
-            dma((2, 4, 3)),
+            dma((2, 4, 3 * SUBS)),
+            dma((2, 3, 3 * SUBS)),
+            dma((2, 3, 3 * SUBS)),
+            dma((2, 3, 3 * SUBS)),
+            dma((2, 3, 3 * SUBS)),
+            dma((2, 3, 3 * SUBS)),
+            dma((2, 3, 3 * SUBS)),
+            dma((2, 4, 3 * SUBS)),
             dma((4,)),
         ]
         + [pltpu.VMEM((32, CR, C), BF16)] * NCH,
@@ -595,62 +614,105 @@
     )(tile_mask, source_owner, source_block, margin_weight, grid, teacher, conv, mix)
 
 
-def place_kernel(mask, next_in, mis_in, conv_in, mix_in, next_ref, mis_ref, conv_ref, mix_ref):
-    i = pl.program_id(0)
-    slot = jnp.int32(0)
-    for j in range(8):
-        slot = slot + jnp.where(j < i, mask[j], 0)
-    slot = jnp.minimum(slot, SLOTS - 1)
-    ocean = mask[i] == 1
-
-    @pl.when(ocean)
-    def _():
-        next_ref[...] = next_in[slot].reshape(TS, TS, C)
-        mis_ref[...] = mis_in[slot].reshape(TS, TS, C)
-
-    @pl.when(jnp.logical_not(ocean))
-    def _():
-        next_ref[...] = jnp.zeros_like(next_ref)
-        mis_ref[...] = jnp.zeros_like(mis_ref)
-
-    conv_ref[...] = conv_in[...].astype(F32)
-    mix_ref[...] = mix_in[...].astype(F32)
+def place_kernel(
+    mask, next_in, mis_in, conv_in, mix_in, next_out, mis_out, conv_out, mix_out,
+    next_buf, mis_buf, conv_buf, mix_buf, conv_wide, mix_wide, zero, sem_in, sem_conv, sem_out, sem_wide,
+):
+    loads = [
+        pltpu.make_async_copy(next_in, next_buf, sem_in.at[0]),
+        pltpu.make_async_copy(mis_in, mis_buf, sem_in.at[1]),
+        pltpu.make_async_copy(mix_in, mix_buf, sem_in.at[2]),
+    ]
+    steps = [pltpu.make_async_copy(conv_in.at[n], conv_buf.at[n], sem_conv.at[n]) for n in range(9)]
+    for copy in [steps[0]] + loads + steps[1:]:
+        copy.start()
+    zero[...] = jnp.zeros_like(zero)
+    outs = []
+
+    def tiles(kind, buf, out):
+        loads[kind].wait()
+        slot = jnp.int32(0)
+        for i in range(8):
+            a, b = i // 2, i % 2
+            spot = out.at[a * TS : (a + 1) * TS, b * TS : (b + 1) * TS]
+            done = sem_out.at[kind, i]
+            real = pltpu.make_async_copy(buf.at[jnp.minimum(slot, SLOTS - 1)], spot, done)
+            blank = pltpu.make_async_copy(zero, spot, done)
+
+            @pl.when(mask[0, 0, i] == 1)
+            def _(real=real):
+                real.start()
+
+            @pl.when(mask[0, 0, i] != 1)
+            def _(blank=blank):
+                blank.start()
+
+            slot = slot + mask[0, 0, i]
+            outs.append(blank)
+
+    def widen(n):
+        steps[n].wait()
+        conv_wide[n] = conv_buf[n].astype(F32)
+        copy = pltpu.make_async_copy(conv_wide.at[n], conv_out.at[n], sem_wide.at[n])
+        copy.start()
+        outs.append(copy)
+
+    widen(0)
+    tiles(0, next_buf, next_out)
+    widen(1)
+    tiles(1, mis_buf, mis_out)
+    for n in range(2, 9):
+        widen(n)
+    loads[2].wait()
+    mix_wide[...] = mix_buf[...].astype(F32)
+    copy = pltpu.make_async_copy(mix_wide, mix_out, sem_wide.at[9])
+    copy.start()
+    outs.append(copy)
+    for copy in outs:
+        copy.wait()
 
 
 def place_tiles(mask, next_in, mis_in, conv_in, mix_in):
-    tile = pl.BlockSpec((TS, TS, C), lambda i, mask: (i // 2, i % 2, 0))
-    whole = pl.BlockSpec((SLOTS, 256, C), lambda i, mask: (0, 0, 0))
-    conv = pl.BlockSpec((9 * C // 8, C), lambda i, mask: (i, 0))
-    mix = pl.BlockSpec((C // 8, C), lambda i, mask: (i, 0))
+    anywhere = pl.BlockSpec(memory_space=pl.ANY)
+    dma = pltpu.SemaphoreType.DMA
+    tiles = (SLOTS, TS, TS, C)
     return pl.pallas_call(
         place_kernel,
         out_shape=(
             jax.ShapeDtypeStruct((64, 32, C), BF16),
             jax.ShapeDtypeStruct((64, 32, C), BF16),
-            jax.ShapeDtypeStruct((9 * C, C), F32),
+            jax.ShapeDtypeStruct((9, C, C), F32),
             jax.ShapeDtypeStruct((C, C), F32),
         ),
-        grid_spec=pltpu.PrefetchScalarGridSpec(
-            num_scalar_prefetch=1,
-            grid=(8,),
-            in_specs=[whole, whole, conv, mix],
-            out_specs=(tile, tile, conv, mix),
-        ),
-        compiler_params=pltpu.CompilerParams(dimension_semantics=("arbitrary",)),
-    )(mask, next_in, mis_in, conv_in, mix_in)
+        in_specs=[pl.BlockSpec(memory_space=pltpu.SMEM)] + [anywhere] * 4,
+        out_specs=(anywhere,) * 4,
+        scratch_shapes=[
+            pltpu.VMEM(tiles, BF16),
+            pltpu.VMEM(tiles, BF16),
+            pltpu.VMEM((9, C, C), BF16),
+            pltpu.VMEM((C, C), BF16),
+            pltpu.VMEM((9, C, C), F32),
+            pltpu.VMEM((C, C), F32),
+            pltpu.VMEM((TS, TS, C), BF16),
+            dma((3,)),
+            dma((9,)),
+            dma((2, 8)),
+            dma((10,)),
+        ],
+    )(mask, next_in.reshape(tiles), mis_in.reshape(tiles), conv_in.reshape(9, C, C), mix_in)
 
 
 def body(
     grid_state, conv_weight, mix_weight, teacher, tile_mask, source_owner, source_block, margin_weight
 ):
-    width_lon, width_lat, chans = grid_state.shape
+    width_lon, width_lat, _ = grid_state.shape
     cells = width_lon * lax.axis_size("lon") * width_lat * lax.axis_size("lat")
     parts = step(
         tile_mask, source_owner, source_block, margin_weight, grid_state, teacher,
         conv_weight, mix_weight, 1.0 / math.sqrt(cells),
     )
-    next_state, misfit, grad_conv, grad_mix = place_tiles(tile_mask.reshape(8), *parts)
-    return next_state, misfit, grad_conv.reshape(9, chans, chans), grad_mix
+    next_state, misfit, grad_conv, grad_mix = place_tiles(tile_mask, *parts)
+    return next_state, misfit, grad_conv, grad_mix
 
 
 def solution(mesh):

time: 125 us -> 113 us (0.904)
  Pallas kernels: 124 us -> 112 us
    pallas_call x1, Pallas kernels: 116 us -> 106 us  [step(): pl.pallas_call(functools.partial(step_kernel, scale=scale), out_shape=(ja...]
    pallas_call x1, Pallas kernels: 8.34 us -> 5.95 us  [place_tiles(): pl.pallas_call(place_kernel, out_shape=(jax.ShapeDtypeStruct((64, 32, C),...]
where the time goes in v3:
time: 113 us
  Pallas kernels  112 us (99%)
    pallas_call x1, Pallas kernels, step(): pl.pallas_call(functools.partial(step_kernel, scale=scale), out_shape=(ja...  106 us
    pallas_call x1, Pallas kernels, place_tiles(): pl.pallas_call(place_kernel, out_shape=(jax.ShapeDtypeStruct((64, 32, C),...  5.95 us

profile of v3, /device:TPU:1, one launch (start us, length us, event | category | flops | bytes accessed | tf_op | source)
XLA Modules:
  0.0 113.2 jit_solution(13056705880607257449)
XLA Ops:
  0.6 106.5 %shard_map.111 = (bf16[4,256,384]{2,1,0:T(8,128)(2,1)}, bf16[4,256,384]{2,1,0:T(8,128)(2,1)}, bf16[3456,384]{1,0:T(8,128)(2,1)}, bf16[384,384]{1,0:T(8,128)(2,1)}) custom-call(s32[1,1,8]{2,1,0:T(1,128)} %mask.1, s32[1,16,16]{2,1,0:T(8,128)} %owner_ref.1, s32[1,16,16]{2,1,0:T(8,128)} %block_ref.1, f32[1,1,16]{2,1,0:T(1,128)} %margin_ref.1, ...), custom_call_target="tpu_custom_call" | custom-call | tf_op jit(solution)/shard_map/pallas_call | solution.py:548
  107.1 6.0 %shard_map.112 = (bf16[64,32,384]{2,1,0:T(8,128)(2,1)}, bf16[64,32,384]{2,1,0:T(8,128)(2,1)}, f32[9,384,384]{2,1,0:T(8,128)}, f32[384,384]{1,0:T(8,128)}) custom-call(s32[1,1,8]{2,1,0:T(1,128)} %mask.1, bf16[4,16,16,384]{3,2,1,0:T(8,128)(2,1)} %bitcast.4, bf16[4,16,16,384]{3,2,1,0:T(8,128)(2,1)} %bitcast.5, bf16[9,384,384]{2,1,0:T(8,128)(2,1)} %bitcast.3, ...), custom_call_target="tpu_custom_call" | custom-call | tf_op jit(solution)/shard_map/pallas_call | solution.py:679

commit v4 on v3

--- a/solution.py
+++ b/solution.py
@@ -54,12 +54,12 @@
 
 def step_kernel(
     mask_ref, owner_ref, block_ref, margin_ref, grid, teacher, conv, mix,
-    next_out, mis_out, conv_out, mix_out,
+    next_out, mis_out, total_out,
     mi_own, mw_own, mi_buf, mw_buf, mi_smem, mw_smem, send, sums,
     pad, lat_buf, cor_buf, edge, wbuf, mbuf, xs, pre_buf, full_buf, hid, sc, dp, next_buf, mis_buf,
     grads, gb, rc, s1, r1, a1, r2, a2, r3, obuf,
     sem_in, sem_m, sem_ms, sem_h, sem_own, sem_core, sem_far, sem_x1, sem_x0,
-    sem_c, sem_1, sem_2, sem_3, sem_g3, sem_g2, sem_g1, sem_gc, sem_o, *raw,
+    sem_c, sem_1, sem_2, sem_3, sem_g3, sem_g2, sem_g1, sem_gc, sem_o, sem_k, *raw,
     scale,
 ):
     x, y, z, core = my_place()
@@ -124,7 +124,6 @@
             ).wait_recv()
 
     start_far(0)
-    start_far(1)
 
     count = jnp.int32(0)
     chosen = []
@@ -180,8 +179,6 @@
                 partner,
             )
         )
-    start_far(2)
-
     loads[0].wait()
     spot = lax.broadcasted_iota(jnp.int32, (64, 1024), 1)
     line = lax.broadcasted_iota(jnp.int32, (64, 1024), 0) * 16
@@ -200,6 +197,7 @@
         )
     ):
         halos.append(go(remote(src, dst, sem_h.at[0, n], sem_h.at[1, n], where)))
+    start_far(1)
     for s in range(4):
         for c in (0, 1):
             if s == 0 and c == 1:
@@ -339,17 +337,17 @@
 
     for ch in range(NCH):
         weigh(ch)
-        if ch + 3 < NCH:
-            start_far(ch + 3)
+        if ch + 2 < NCH:
+            start_far(ch + 2)
         start_x(ch)
-        if ch == 0:
+        if ch == 1:
             corners()
-        elif ch == 1:
+        elif ch == 3:
             windows()
-        elif ch < SLOTS + 2:
-            forward(ch - 2)
-
-    for ch in range(NCH):
+        for t in {4: (0,), 5: (1,), 6: (2,), 7: (3,)}.get(ch, ()):
+            forward(t)
+
+    def sums_arrived(ch):
         for h in (0, 1):
             for d in (1, 2, 3):
                 remote(
@@ -368,45 +366,68 @@
         ).wait_recv()
         own[ch, "x"].wait()
 
-    def backward(t, carry):
-        pre = pre_buf[t]
-        sig = jax.nn.sigmoid(pre)
-        target = sums[0, t].astype(F32)
-        for n in range(1, 4):
-            target = target + sums[n, t].astype(F32)
-        error = (full_buf[t] - target) * (t < count).astype(F32)
-        mis_buf[t] = error.astype(BF16)
-        scaled = (error * scale).astype(BF16)
-        back = lax.dot_general(
-            scaled, mbuf[...], (((1,), (1,)), ((), ())), preferred_element_type=F32
-        )
-        sc[t] = scaled
-        dp[t] = (back * sig * (1.0 + pre * (1.0 - sig))).astype(BF16)
-        return carry
-
-    lax.fori_loop(0, SLOTS, backward, 0)
-    outs = [
-        pltpu.make_async_copy(next_buf, next_out, sem_o.at[0]),
-        pltpu.make_async_copy(mis_buf, mis_out, sem_o.at[1]),
-    ]
-    for copy in outs:
-        copy.start()
+    def backward(t, lo, n):
+        for h in (0, 1):
+            at = slice(h * 128 + lo, h * 128 + lo + n)
+            pre = pre_buf[t, at]
+            sig = jax.nn.sigmoid(pre)
+            target = sums[0, t, at].astype(F32)
+            for m in range(1, 4):
+                target = target + sums[m, t, at].astype(F32)
+            error = (full_buf[t, at] - target) * (t < count).astype(F32)
+            mis_buf[t, at] = error.astype(BF16)
+            scaled = (error * scale).astype(BF16)
+            back = lax.dot_general(
+                scaled, mbuf[...], (((1,), (1,)), ((), ())), preferred_element_type=F32
+            )
+            sc[t, at] = scaled
+            dp[t, at] = (back * sig * (1.0 + pre * (1.0 - sig))).astype(BF16)
 
     contract = (((0,), (0,)), ((), ()))
-    for tap in range(10):
-        lon_step, lat_step = divmod(tap, 3)
-        if tap < 9:
-            left = jnp.concatenate(
-                [xs[lat_step, tile, lon_step * 16 : lon_step * 16 + 256, :] for tile in tiles]
-            )
-            right = dp[...].reshape(1024, C)
-        else:
-            left, right = hid[...].reshape(1024, C), sc[...].reshape(1024, C)
-        grad = lax.dot_general(left, right, contract, preferred_element_type=F32)
-        grads[tap * C : (tap + 1) * C, :] = grad
-        gb[tap * C : (tap + 1) * C, :] = grad.astype(BF16)
+
+    def gradients(lo, n, more):
+        picks = [(t, h * 128 + lo) for t in range(SLOTS) for h in (0, 1)]
+
+        def gather(ref):
+            return jnp.concatenate([ref[t, at : at + n] for t, at in picks])
+
+        right = gather(dp)
+        for tap in range(10):
+            lon_step, lat_step = divmod(tap, 3)
+            if tap < 9:
+                left = jnp.concatenate(
+                    [
+                        xs[lat_step, tiles[t], lon_step * 16 + at : lon_step * 16 + at + n, :]
+                        for t, at in picks
+                    ]
+                )
+            else:
+                left, right = gather(hid), gather(sc)
+            grad = lax.dot_general(left, right, contract, preferred_element_type=F32)
+            span = slice(tap * C, (tap + 1) * C)
+            if more:
+                grads[span] = grad
+            else:
+                grad = grads[span] + grad
+                grads[span] = grad
+                gb[span] = grad.astype(BF16)
+
+    outs = [pltpu.make_async_copy(next_buf, next_out, sem_o.at[0])]
+    outs[0].start()
     grads[10 * C : 2 * HALF, :] = jnp.zeros((2 * HALF - 10 * C, C), F32)
     gb[10 * C : 2 * HALF, :] = jnp.zeros((2 * HALF - 10 * C, C), BF16)
+    for start, end, more in ((0, NCH - 2, True), (NCH - 2, NCH, False)):
+        for ch in range(start, end):
+            sums_arrived(ch)
+
+        def each(t, carry, lo=start * CR, n=(end - start) * CR):
+            backward(t, lo, n)
+            return carry
+
+        lax.fori_loop(0, SLOTS, each, 0)
+        gradients(start * CR, (end - start) * CR, more)
+    outs.append(pltpu.make_async_copy(mis_buf, mis_out, sem_o.at[1]))
+    outs[1].start()
 
     def col(q):
         return pl.ds(q * 128, 128)
@@ -512,8 +533,20 @@
             g3[p][r].wait_recv()
         g2[p] = spread(p, 2, sem_g2)
 
+    def keep(half, p, r):
+        piece = half_span(half, p, r)
+        copy = pltpu.make_async_copy(obuf.at[piece], total_out.at[piece], sem_k.at[half, r, p])
+        copy.start()
+        outs.append(copy)
+
+    def half_span(half, p, r):
+        start = core if half == 0 else other
+        start = start * HALF + (p // 3) * (HALF // SUBS) + lax.rem(place[p % 3] + r, 4) * PIECE
+        return pl.ds(pl.multiple_of(start, PIECE), PIECE), col(p % 3)
+
     def give(p, r):
         piece = obuf.at[span(p, 1, r)]
+        keep(0, p, r)
         gc[p, r] = go(remote(piece, piece, sem_gc.at[0, r, p], sem_gc.at[1, r, p], partner))
 
     for p in parts:
@@ -526,15 +559,11 @@
             for p in group:
                 g1[p][r].wait_recv()
                 give(p, 4 - r)
-    for r in range(4):
-        for p in parts:
-            gc[p, r].wait_recv()
-    outs += [
-        pltpu.make_async_copy(obuf.at[0 : 9 * C], conv_out, sem_o.at[2]),
-        pltpu.make_async_copy(obuf.at[9 * C : 10 * C], mix_out, sem_o.at[3]),
-    ]
-    for copy in outs[2:]:
-        copy.start()
+    for group in groups:
+        for r in (0, 3, 1, 2):
+            for p in group:
+                gc[p, r].wait_recv()
+                keep(1, p, r)
     for copy in pend:
         copy.wait_send()
     for copy in outs:
@@ -550,11 +579,10 @@
         out_shape=(
             jax.ShapeDtypeStruct((SLOTS, 256, C), BF16),
             jax.ShapeDtypeStruct((SLOTS, 256, C), BF16),
-            jax.ShapeDtypeStruct((9 * C, C), BF16),
-            jax.ShapeDtypeStruct((C, C), BF16),
+            jax.ShapeDtypeStruct((2 * HALF, C), BF16),
         ),
         in_specs=[smem] * 4 + [anywhere] * 4,
-        out_specs=(anywhere,) * 4,
+        out_specs=(anywhere,) * 3,
         scratch_shapes=[
             pltpu.VMEM((1, 128), jnp.int32),
             pltpu.VMEM((1, 128), F32),
@@ -605,7 +633,8 @@
             dma((2, 3, 3 * SUBS)),
             dma((2, 3, 3 * SUBS)),
             dma((2, 4, 3 * SUBS)),
-            dma((4,)),
+            dma((2,)),
+            dma((2, 4, 3 * SUBS)),
         ]
         + [pltpu.VMEM((32, CR, C), BF16)] * NCH,
         compiler_params=pltpu.CompilerParams(
@@ -615,15 +644,18 @@
 
 
 def place_kernel(
-    mask, next_in, mis_in, conv_in, mix_in, next_out, mis_out, conv_out, mix_out,
+    mask, next_in, mis_in, total, next_out, mis_out, conv_out, mix_out,
     next_buf, mis_buf, conv_buf, mix_buf, conv_wide, mix_wide, zero, sem_in, sem_conv, sem_out, sem_wide,
 ):
     loads = [
         pltpu.make_async_copy(next_in, next_buf, sem_in.at[0]),
         pltpu.make_async_copy(mis_in, mis_buf, sem_in.at[1]),
-        pltpu.make_async_copy(mix_in, mix_buf, sem_in.at[2]),
+        pltpu.make_async_copy(total.at[9 * C : 10 * C], mix_buf, sem_in.at[2]),
     ]
-    steps = [pltpu.make_async_copy(conv_in.at[n], conv_buf.at[n], sem_conv.at[n]) for n in range(9)]
+    steps = [
+        pltpu.make_async_copy(total.at[n * C : (n + 1) * C], conv_buf.at[n], sem_conv.at[n])
+        for n in range(9)
+    ]
     for copy in [steps[0]] + loads + steps[1:]:
         copy.start()
     zero[...] = jnp.zeros_like(zero)
@@ -672,7 +704,7 @@
         copy.wait()
 
 
-def place_tiles(mask, next_in, mis_in, conv_in, mix_in):
+def place_tiles(mask, next_in, mis_in, total):
     anywhere = pl.BlockSpec(memory_space=pl.ANY)
     dma = pltpu.SemaphoreType.DMA
     tiles = (SLOTS, TS, TS, C)
@@ -684,7 +716,7 @@
             jax.ShapeDtypeStruct((9, C, C), F32),
             jax.ShapeDtypeStruct((C, C), F32),
         ),
-        in_specs=[pl.BlockSpec(memory_space=pltpu.SMEM)] + [anywhere] * 4,
+        in_specs=[pl.BlockSpec(memory_space=pltpu.SMEM)] + [anywhere] * 3,
         out_specs=(anywhere,) * 4,
         scratch_shapes=[
             pltpu.VMEM(tiles, BF16),
@@ -699,7 +731,7 @@
             dma((2, 8)),
             dma((10,)),
         ],
-    )(mask, next_in.reshape(tiles), mis_in.reshape(tiles), conv_in.reshape(9, C, C), mix_in)
+    )(mask, next_in.reshape(tiles), mis_in.reshape(tiles), total)
 
 
 def body(

time: 113 us -> 105 us (0.929)
  Pallas kernels: 112 us -> 104 us
    pallas_call x1, Pallas kernels: 106 us -> 97.8 us  [step(): pl.pallas_call(functools.partial(step_kernel, scale=scale), out_shape=(ja...]
where the time goes in v4:
time: 105 us
  Pallas kernels  104 us (99%)
    pallas_call x1, Pallas kernels, step(): pl.pallas_call(functools.partial(step_kernel, scale=scale), out_shape=(ja...  97.8 us
    pallas_call x1, Pallas kernels, place_tiles(): pl.pallas_call(place_kernel, out_shape=(jax.ShapeDtypeStruct((64, 32, C),...  5.95 us

profile of v4, /device:TPU:1, one launch (start us, length us, event | category | flops | bytes accessed | tf_op | source)
XLA Modules:
  0.0 104.5 jit_solution(2746906739181486514)
XLA Ops:
  0.6 97.8 %shard_map.111 = (bf16[4,256,384]{2,1,0:T(8,128)(2,1)}, bf16[4,256,384]{2,1,0:T(8,128)(2,1)}, bf16[4096,384]{1,0:T(8,128)(2,1)}) custom-call(s32[1,1,8]{2,1,0:T(1,128)} %mask.1, s32[1,16,16]{2,1,0:T(8,128)} %owner_ref.1, s32[1,16,16]{2,1,0:T(8,128)} %block_ref.1, f32[1,1,16]{2,1,0:T(1,128)} %margin_ref.1, bf16[64,32,384]{2,1,0:T(8,128)(2,1)} %grid.1, ...), custom_call_target="tpu_custom_call" | custom-call | tf_op jit(solution)/shard_map/pallas_call | solution.py:577
  98.4 6.0 %shard_map.112 = (bf16[64,32,384]{2,1,0:T(8,128)(2,1)}, bf16[64,32,384]{2,1,0:T(8,128)(2,1)}, f32[9,384,384]{2,1,0:T(8,128)}, f32[384,384]{1,0:T(8,128)}) custom-call(s32[1,1,8]{2,1,0:T(1,128)} %mask.1, bf16[4,16,16,384]{3,2,1,0:T(8,128)(2,1)} %bitcast.2, bf16[4,16,16,384]{3,2,1,0:T(8,128)(2,1)} %bitcast.3, bf16[4096,384]{1,0:T(8,128)(2,1)} %get-tuple-element.9.total), custom_call_target="tpu_custom_call" | custom-call | tf_op jit(solution)/shard_map/pallas_call | solution.py:711

commit v5 on v4

--- a/solution.py
+++ b/solution.py
@@ -344,7 +344,7 @@
             corners()
         elif ch == 3:
             windows()
-        for t in {4: (0,), 5: (1,), 6: (2,), 7: (3,)}.get(ch, ()):
+        for t in {5: (0,), 6: (1,), 7: (2, 3)}.get(ch, ()):
             forward(t)
 
     def sums_arrived(ch):

time: 105 us -> 107 us (1.019)
  Pallas kernels: 104 us -> 106 us
    pallas_call x1, Pallas kernels: 97.8 us -> 99.8 us  [step(): pl.pallas_call(functools.partial(step_kernel, scale=scale), out_shape=(ja...]
where the time goes in v5:
time: 107 us
  Pallas kernels  106 us (99%)
    pallas_call x1, Pallas kernels, step(): pl.pallas_call(functools.partial(step_kernel, scale=scale), out_shape=(ja...  99.8 us
    pallas_call x1, Pallas kernels, place_tiles(): pl.pallas_call(place_kernel, out_shape=(jax.ShapeDtypeStruct((64, 32, C),...  5.95 us

profile of v5, /device:TPU:1, one launch (start us, length us, event | category | flops | bytes accessed | tf_op | source)
XLA Modules:
  0.0 106.6 jit_solution(16646690098452844376)
XLA Ops:
  0.6 99.8 %shard_map.111 = (bf16[4,256,384]{2,1,0:T(8,128)(2,1)}, bf16[4,256,384]{2,1,0:T(8,128)(2,1)}, bf16[4096,384]{1,0:T(8,128)(2,1)}) custom-call(s32[1,1,8]{2,1,0:T(1,128)} %mask.1, s32[1,16,16]{2,1,0:T(8,128)} %owner_ref.1, s32[1,16,16]{2,1,0:T(8,128)} %block_ref.1, f32[1,1,16]{2,1,0:T(1,128)} %margin_ref.1, bf16[64,32,384]{2,1,0:T(8,128)(2,1)} %grid.1, ...), custom_call_target="tpu_custom_call" | custom-call | tf_op jit(solution)/shard_map/pallas_call | solution.py:577
  100.5 6.0 %shard_map.112 = (bf16[64,32,384]{2,1,0:T(8,128)(2,1)}, bf16[64,32,384]{2,1,0:T(8,128)(2,1)}, f32[9,384,384]{2,1,0:T(8,128)}, f32[384,384]{1,0:T(8,128)}) custom-call(s32[1,1,8]{2,1,0:T(1,128)} %mask.1, bf16[4,16,16,384]{3,2,1,0:T(8,128)(2,1)} %bitcast.2, bf16[4,16,16,384]{3,2,1,0:T(8,128)(2,1)} %bitcast.3, bf16[4096,384]{1,0:T(8,128)(2,1)} %get-tuple-element.9.total), custom_call_target="tpu_custom_call" | custom-call | tf_op jit(solution)/shard_map/pallas_call | solution.py:711
